TPU v7x, 32 devices: a whole 2x2x4 slice. The times are simulated.
32 devices in a mesh: row: 8 (over y, x, core), col: 4 (over z).
Axes of the slice: x: 2, y: 2, z: 4, core: 2. Of those that a mesh axis runs over, the one named last changes fastest.
Arguments:
- upper_s: float32 [4, 2048, 8, 1024], P(None, 'row', None, 'col')
- upper_t: float32 [4, 2048, 8, 1024], P(None, 'row', None, 'col')
- left_vectors: float32 [4, 2048, 8, 1024], P(None, 'row', None, 'col'), may hold values from -6 to 6
- right_vectors: float32 [4, 2048, 8, 1024], P(None, 'row', None, 'col'), may hold values from -6 to 6
- window_starts: int32 [3, 16], replicated, may hold values from 0 to 31, as said below
- selection: int32 [3, 16, 256], replicated, may hold values 0 or 1
- window_factors: float32 [3, 16, 2, 256, 256], P(None, 'row')
Outputs:
- new_s: float32 [4, 2048, 8, 1024], P(None, 'row', None, 'col')
- new_t: float32 [4, 2048, 8, 1024], P(None, 'row', None, 'col')
- new_left: float32 [4, 2048, 8, 1024], P(None, 'row', None, 'col')
- new_right: float32 [4, 2048, 8, 1024], P(None, 'row', None, 'col')
Inputs may be any that keep to these rules, and one draw needn't show every extreme that they name: `window_starts`: within each round the 16 block numbers are distinct.
All inputs are finite; a program needn't handle non-finite values.
Results may differ from a plain program's by a relative error of at most 0.0001.
Values sent between devices are 32-bit elements; how exact they have to be, the bound alone decides.
No kernel may reach another device: no remote copies, remote signals or barrier semaphores. Data moves between devices by JAX's collectives and lax.ppermute only.
A program may use at most 192 MiB of HBM per device.

v0:
```python
import functools
import math

import jax
import jax.numpy as jnp
import numpy as np
from jax import lax
from jax.experimental import pallas as pl
from jax.experimental.pallas import tpu as pltpu
from jax.sharding import PartitionSpec as P


F32 = jnp.float32
BF16 = jnp.bfloat16
LANES = 128
MIB = 1 << 20
ANY = pl.BlockSpec(memory_space=pl.ANY)
SMEM = pl.BlockSpec(memory_space=pltpu.SMEM)
VMEM = pl.BlockSpec(memory_space=pltpu.VMEM)


def halves(x):
    high = x.astype(BF16)
    return high, (x - high.astype(F32)).astype(BF16)


def dot(a, b):
    return jnp.dot(a, b, preferred_element_type=F32)


def dot_nt(a, b):
    return lax.dot_general(a, b, (((1,), (1,)), ((), ())), preferred_element_type=F32)


def product(a, b):
    return dot(a[0], b[0]) + (dot(a[0], b[1]) + dot(a[1], b[0]))


class Plan:
    def __init__(self, rows, cols, row_blocks, col_blocks, rounds, own, width):
        assert rows >= 4 and rows & (rows - 1) == 0
        self.rows, self.cols, self.row_blocks, self.col_blocks = rows, cols, row_blocks, col_blocks
        self.rounds, self.own, self.width, self.parts = rounds, own, width, width // LANES
        self.blocks = row_blocks * rows
        self.nodes = rows // 2
        self.stages = self.nodes.bit_length() - 1
        self.col_units = max(1, col_blocks // self.nodes)
        self.row_units = -(-row_blocks // cols)
        self.units = self.col_units + self.row_units
        self.slots = self.nodes * self.units * rounds
        self.most = [(self.nodes >> (t + 1)) * self.units * rounds for t in range(self.stages)]
        means = [m * own * rows / self.blocks * 2**t / self.nodes for t, m in enumerate(self.most)]
        self.cap = [min(m, max(1, math.ceil(x + 2.5 * math.sqrt(x)))) for m, x in zip(self.most, means)]

    def bit(self, t, core):
        return jnp.where(core == 0, 1 << (t % self.stages), 1 << ((t + 1) % self.stages))

    def mask(self, first, last, core):
        total = 0
        for t in range(first, last):
            total = total + self.bit(t, core)
        return total

    def turn(self, t):
        pairs = []
        for row in range(self.rows):
            shift = t % self.stages if row % 2 == 0 else (t + 1) % self.stages
            pairs.append((row, row ^ (2 << shift)))
        return pairs

    def swap(self):
        return [(row, row ^ 1) for row in range(self.rows)]

    def block_of(self, node, unit, core, col):
        first = ((node * self.col_blocks) // self.nodes + unit) * self.cols + col
        part = col * self.row_units + unit - self.col_units
        second = part * self.rows + 2 * node + core
        is_col = unit < self.col_units
        return is_col, jnp.where(is_col, first, jnp.clip(second, 0, self.blocks - 1)), is_col | (part < self.row_blocks)

    def present(self, t, here, node, owner, core):
        diff, away = node ^ here, owner ^ here
        ahead = (diff & self.mask(0, t, core)) == 0
        return ahead & ((diff & self.bit(t, core)) != 0) & ((away & self.mask(t, self.stages, core)) == 0)

    def overflows(self, starts):
        axes = (self.stages, 2, self.cols, self.nodes)
        stage, core, col, here = (x.reshape(-1, 1) for x in np.indices(axes).astype(np.int32))
        bits = np.array([[1 << ((t + c) % self.stages) for c in range(2)] for t in range(self.stages)], np.int32)
        before = np.array([[bits[:t, c].sum() for c in range(2)] for t in range(self.stages)], np.int32)[stage, core]
        now, after = bits[stage, core], (self.nodes - 1) & ~before
        block = starts.reshape(1, -1)
        windows = jnp.arange(starts.shape[1], dtype=jnp.int32) // (2 * self.own)
        owner = jnp.tile(windows, starts.shape[0]).reshape(1, -1)
        mine = ((owner ^ here) & after) == 0
        copies = max(1, self.nodes // self.col_blocks)
        total = 0
        for copy in range(copies):
            node = (block // self.cols // self.col_units) * copies + copy
            on = (block % self.cols == col) & (((node ^ here) & before) == 0) & (((node ^ here) & now) != 0)
            total = total + (on & mine).astype(jnp.int32)
        row, part = block % self.rows, block // self.rows
        node = row // 2
        on = (part // self.row_units == col) & (row % 2 == core)
        on = on & (((node ^ here) & before) == 0) & (((node ^ here) & now) != 0)
        total = total + (on & mine).astype(jnp.int32)
        counts = jnp.sum(total, axis=1).reshape(self.stages, -1)
        return jnp.max(counts, axis=1) > jnp.array(self.cap, jnp.int32)


SHIFT = 12


class Walk:
    def __init__(self, plan, meta, inv, stage, table):
        self.plan, self.inv, self.stage = plan, inv, stage
        self.row, self.col = meta[0], meta[1]
        self.core, self.here = self.row % 2, self.row // 2
        self.table = table
        for t in range(stage):
            self.scan(t, self.here ^ plan.bit(t, self.core), functools.partial(self.note, t))

    def note(self, t, slot, count, info):
        self.table[t, slot] = count

    def info(self, slot):
        plan = self.plan
        node = slot // (plan.units * plan.rounds)
        unit = (slot // plan.rounds) % plan.units
        turn = slot % plan.rounds
        is_col, block, valid = plan.block_of(node, unit, self.core, self.col)
        window = jnp.where(valid, self.inv[turn, block], -1)
        side = jnp.where(is_col, self.core, 0)
        return node, turn, window, side

    def scan(self, t, here, act):
        def step(slot, count):
            info = self.info(slot)
            owner = jnp.maximum(info[2], 0) // (2 * self.plan.own)
            hit = (info[2] >= 0) & self.plan.present(t, here, info[0], owner, self.core)

            @pl.when(hit)
            def _():
                act(slot, count, info)

            return count + hit.astype(jnp.int32)

        return lax.fori_loop(0, self.plan.slots, step, jnp.int32(0))

    def source(self, slot, info):
        plan = self.plan
        _, turn, window, side = info
        row = window // plan.own
        away = (row // 2) ^ self.here
        code = ((row != self.row).astype(jnp.int32) << SHIFT) + (turn * plan.own + window % plan.own) * 2 + side
        for t in range(self.stage):
            place = self.table[t, slot]
            rest = place >= plan.cap[t]
            there = ((2 + 2 * t + rest.astype(jnp.int32)) << SHIFT) + place - jnp.where(rest, plan.cap[t], 0)
            code = jnp.where((away & plan.bit(t, self.core)) != 0, there, code)
        return code


def route_kernel(plan, t, meta, inv, jobs, table):
    walk = Walk(plan, meta, inv, t, table)
    if t < plan.stages:

        def act(slot, count, info):
            jobs[1 + count] = walk.source(slot, info)

        jobs[0] = walk.scan(t, walk.here, act)
        return
    places = plan.units * plan.rounds

    def step(place, carry):
        slot = walk.here * places + place
        info = walk.info(slot)
        jobs[places + place] = info[2]
        jobs[place] = walk.source(slot, (info[0], info[1], jnp.maximum(info[2], 0), info[3]))
        return carry

    lax.fori_loop(0, places, step, 0)


def route(plan, t, meta, inv):
    size = 1 + plan.most[t] if t < plan.stages else 2 * plan.units * plan.rounds
    return pl.pallas_call(
        functools.partial(route_kernel, plan, t),
        in_specs=[SMEM, SMEM],
        out_specs=SMEM,
        out_shape=jax.ShapeDtypeStruct((size,), jnp.int32),
        scratch_shapes=[pltpu.SMEM((max(1, t), plan.slots), jnp.int32)],
        compiler_params=pltpu.CompilerParams(vmem_limit_bytes=MIB),
    )(meta, inv)


def fetch(code, sources, target, sem):
    for number, ref in enumerate(sources):

        @pl.when((code >> SHIFT) == number)
        def _(ref=ref):
            pltpu.make_async_copy(ref.at[code & ((1 << SHIFT) - 1)], target, sem).start()


def arrived(sources, target, sem):
    pltpu.make_async_copy(sources[0].at[0], target, sem).wait()


def pack_kernel(plan, t, jobs, *refs):
    sources, (first, rest, spill, sems, spill_sem) = refs[: 2 + 2 * t], refs[2 + 2 * t :]
    cap = plan.cap[t]
    count = jobs[0]

    def begin(place, carry):
        fetch(jobs[1 + place], sources, first.at[place], sems.at[place])
        return carry

    def settle(place, carry):
        arrived(sources, first.at[place], sems.at[place])
        return carry

    def over(place, carry):
        fetch(jobs[1 + place], sources, spill, spill_sem.at[0])
        arrived(sources, spill, spill_sem.at[0])
        out = pltpu.make_async_copy(spill, rest.at[place - cap], spill_sem.at[1])
        out.start()
        out.wait()
        return carry

    lax.fori_loop(0, jnp.minimum(count, cap), begin, 0)
    lax.fori_loop(cap, count, over, 0)
    lax.fori_loop(0, jnp.minimum(count, cap), settle, 0)


def pack(plan, t, jobs, sources):
    w, cap, rest = plan.width, plan.cap[t], max(1, plan.most[t] - plan.cap[t])
    return pl.pallas_call(
        functools.partial(pack_kernel, plan, t),
        in_specs=[SMEM] + [ANY] * len(sources),
        out_specs=[VMEM, ANY],
        out_shape=[jax.ShapeDtypeStruct((cap, w, w), F32), jax.ShapeDtypeStruct((rest, w, w), F32)],
        scratch_shapes=[
            pltpu.VMEM((w, w), F32),
            pltpu.SemaphoreType.DMA((cap,)),
            pltpu.SemaphoreType.DMA((2,)),
        ],
        compiler_params=pltpu.CompilerParams(vmem_limit_bytes=4 * MIB),
    )(jobs, *placed(sources))


def order(flags):
    width = flags.shape[1]
    row = lax.broadcasted_iota(jnp.int32, (width, width), 0)
    column = lax.broadcasted_iota(jnp.int32, (width, width), 1)
    wide = jnp.broadcast_to(flags, (8, width))
    earlier = dot(wide.astype(BF16), (row < column).astype(F32).astype(BF16))[0:1]
    chosen = jnp.sum(flags, axis=1, keepdims=True)
    position = lax.broadcasted_iota(jnp.int32, (1, width), 1).astype(F32)
    target = jnp.where(flags == 1.0, earlier, chosen + position - earlier)
    return (row.astype(F32) == target).astype(F32).astype(BF16)


def orders_kernel(plan, jobs, flags, out):
    places = plan.units * plan.rounds

    def step(place, carry):
        window = jnp.maximum(jobs[places + place], 0)
        out[place] = order(flags[place % plan.rounds, pl.ds(window, 1), :].astype(F32))
        return carry

    lax.fori_loop(0, places, step, 0)


def orders(plan, jobs, flags):
    return pl.pallas_call(
        functools.partial(orders_kernel, plan),
        in_specs=[SMEM, VMEM],
        out_specs=VMEM,
        out_shape=jax.ShapeDtypeStruct((plan.units * plan.rounds, plan.width, plan.width), BF16),
        compiler_params=pltpu.CompilerParams(vmem_limit_bytes=4 * MIB),
        name="orders",
    )(jobs, flags)


def compose_kernel(plan, jobs, moves, *refs):
    count = 2 + 2 * plan.stages
    sources, (cols, lefts, raw, held, sems) = refs[:count], refs[count:]
    w = plan.width
    places = plan.units * plan.rounds
    for turn in range(plan.rounds):
        for unit in range(plan.units):
            place = unit * plan.rounds + turn

            @pl.when(jobs[places + place] >= 0)
            def _(place=place):
                fetch(jobs[place], sources, raw.at[place], sems.at[place])

    row = lax.broadcasted_iota(jnp.int32, (w, w), 0)
    column = lax.broadcasted_iota(jnp.int32, (w, w), 1)
    unit_matrix = (row == column).astype(F32)
    for turn in range(plan.rounds):
        for unit in range(plan.units):
            place = unit * plan.rounds + turn

            @pl.when(jobs[places + place] >= 0)
            def _(place=place):
                arrived(sources, raw.at[place], sems.at[place])

        for unit in range(plan.units):
            place = unit * plan.rounds + turn
            there = jobs[places + place] >= 0
            factor = halves(jnp.where(there, raw[place], 0.0))
            if turn == 0:
                moved = dot_nt(unit_matrix.astype(BF16), moves[place]).astype(BF16)
                held[unit] = jnp.where(there, dot(moved, factor[0]) + dot(moved, factor[1]), unit_matrix)
            else:
                high, low = halves(held[unit])
                moved = dot_nt(high, moves[place]) + dot_nt(low, moves[place])
                held[unit] = jnp.where(there, product(halves(moved), factor), held[unit])

    for unit in range(plan.col_units):
        cols[unit] = held[unit]
    for unit in range(plan.row_units):
        lefts[unit] = held[plan.col_units + unit]


def compose(plan, jobs, moves, sources):
    w = plan.width
    return pl.pallas_call(
        functools.partial(compose_kernel, plan),
        in_specs=[SMEM, VMEM] + [ANY] * len(sources),
        out_specs=[VMEM, VMEM],
        out_shape=[
            jax.ShapeDtypeStruct((plan.col_units, w, w), F32),
            jax.ShapeDtypeStruct((plan.row_units, w, w), F32),
        ],
        scratch_shapes=[
            pltpu.VMEM((plan.units * plan.rounds, w, w), F32),
            pltpu.VMEM((plan.units, w, w), F32),
            pltpu.SemaphoreType.DMA((plan.units * plan.rounds,)),
        ],
        compiler_params=pltpu.CompilerParams(vmem_limit_bytes=8 * MIB),
        name="compose",
    )(jobs, moves, *placed(sources))


def tiles(plan, act):
    count = plan.row_blocks * plan.col_blocks * plan.parts

    def step(index, carry):
        a, rest = index // (plan.col_blocks * plan.parts), index % (plan.col_blocks * plan.parts)
        act(a, rest // plan.parts, rest % plan.parts)
        return carry

    lax.fori_loop(0, count, step, 0)


def hbm_piece(ref, a, b, p):
    return ref.at[a, :, p, b, 0]


def vmem_piece(ref, a, b, p):
    return ref.at[a, b, :, pl.ds(pl.multiple_of(p * LANES, LANES), LANES)]


def stage_kernel(plan, count, *refs):
    inputs, held, sems = refs[:count], refs[count : 2 * count], refs[2 * count]
    for start in (True, False):
        for m in range(count):

            def act(a, b, p, m=m):
                copy = pltpu.make_async_copy(hbm_piece(inputs[m], a, b, p), vmem_piece(held[m], a, b, p), sems.at[m])
                copy.start() if start else copy.wait()

            tiles(plan, act)


def stage(plan, inputs):
    shape = (plan.row_blocks, plan.col_blocks, plan.width, plan.width)
    count = len(inputs)
    return pl.pallas_call(
        functools.partial(stage_kernel, plan, count),
        in_specs=[ANY] * count,
        out_specs=[VMEM] * count,
        out_shape=[pltpu.VMEM(shape, F32)] * count,
        scratch_shapes=[pltpu.SemaphoreType.DMA((count,))],
        compiler_params=pltpu.CompilerParams(vmem_limit_bytes=MIB),
    )(*in_hbm(inputs))


def combine(plan, m, core):
    offset = 0
    for t in range(plan.stages):
        if (m >> t) & 1:
            offset = offset ^ plan.bit(t, core)
    return offset


def write_out(plan, source, target, b, sem):
    def step(index, carry):
        a, p = index // plan.parts, index % plan.parts
        pltpu.make_async_copy(vmem_piece(source, a, b, p), hbm_piece(target, a, b, p), sem).start()
        return carry

    lax.fori_loop(0, plan.row_blocks * plan.parts, step, 0)


def settle_out(plan, source, target, count, sem):
    def step(index, carry):
        pltpu.make_async_copy(vmem_piece(source, 0, 0, 0), hbm_piece(target, 0, 0, 0), sem).wait()
        return carry

    lax.fori_loop(0, count * plan.row_blocks * plan.parts, step, 0)


def columns(plan, masks, meta, gathered, swapped, data, outputs, high, low, places, sem):
    core, here = meta[0] % 2, meta[0] // 2
    count = jnp.int32(0)
    slots = {}
    for index, m in enumerate(masks):
        node = here ^ combine(plan, m, core)
        base = (node * plan.col_blocks) // plan.nodes
        whole = (node * plan.col_blocks) % plan.nodes == 0
        for unit in range(plan.col_units):
            places[count] = base + unit
            slots[index, unit] = count
            h, l = halves(gathered[index][unit])
            high[core, base + unit] = h
            low[core, base + unit] = l
            count = count + whole.astype(jnp.int32)
        other = here ^ combine(plan, m, 1 - core)
        base = (other * plan.col_blocks) // plan.nodes
        for unit in range(plan.col_units):
            h, l = halves(swapped[index][unit])
            high[1 - core, base + unit] = h
            low[1 - core, base + unit] = l

    def step(index, carry):
        b = places[index]
        for m, kind in ((2, 0), (3, 1), (0, 1), (1, 1)):
            ref = data[m]
            for a in range(plan.row_blocks):
                ref[a, b] = product(halves(ref[a, b]), (high[kind, b], low[kind, b]))
            if m >= 2:
                write_out(plan, ref, outputs[m - 2], b, sem)
        return carry

    lax.fori_loop(0, count, step, 0)
    return count


def early_kernel(plan, masks, extra, meta, *refs):
    n = len(masks)
    gathered, swapped, refs = refs[:n], refs[n : 2 * n], refs[2 * n + 4 + extra :]
    data, outputs, (high, low, places, sem) = refs[:4], refs[4:6], refs[6:]
    count = columns(plan, masks, meta, gathered, swapped, data, outputs, high, low, places, sem)
    settle_out(plan, data[2], outputs[0], 2 * count, sem)


def late_kernel(plan, masks, meta, *refs):
    n, br = len(masks), plan.row_blocks
    gathered, swapped, refs = refs[:n], refs[n : 2 * n], refs[2 * n :]
    lefts, refs = refs[: plan.cols], refs[plan.cols + 6 :]
    data, outputs, refs = refs[:4], refs[4:8], refs[8:]
    high, low, places, left, sem = refs
    w = plan.width
    for shift in range(plan.cols):
        origin = (meta[1] + plan.cols - shift) % plan.cols
        for unit in range(plan.row_units):
            place = origin * plan.row_units + unit

            @pl.when(place < br)
            def _(shift=shift, unit=unit, place=place):
                h, l = halves(lefts[shift][unit].T)
                left[place, pl.ds(0, plan.width)] = h
                left[place, pl.ds(plan.width, plan.width)] = l

    count = columns(plan, masks, meta, gathered, swapped, data, outputs[:2], high, low, places, sem)

    def rows(b, carry):
        for m in range(2):
            for a in range(br):
                y = halves(data[m][a, b])
                both = dot(left[a], y[0])
                data[m][a, b] = both[:w] + (both[w:] + dot(left[a, :w], y[1]))
            write_out(plan, data[m], outputs[2 + m], b, sem)
        return carry

    lax.fori_loop(0, plan.col_blocks, rows, 0)
    settle_out(plan, data[0], outputs[2], 2 * count + 2 * plan.col_blocks, sem)


def held_in_vmem(xs):
    return [pltpu.with_memory_space_constraint(x, pltpu.VMEM) for x in xs]


def placed(sources):
    spaces = [pltpu.VMEM if i >= 2 and i % 2 == 0 else pltpu.HBM for i in range(len(sources))]
    return [pltpu.with_memory_space_constraint(x, space) for x, space in zip(sources, spaces)]


def in_hbm(xs):
    return [pltpu.with_memory_space_constraint(x, pltpu.HBM) for x in xs]


def scratch(plan, limit):
    w, bc = plan.width, plan.col_blocks
    return [
        pltpu.VMEM((2, bc, w, w), BF16),
        pltpu.VMEM((2, bc, w, w), BF16),
        pltpu.SMEM((limit + 1,), jnp.int32),
    ]


def early(plan, masks, meta, gathered, swapped, data, shape, outputs):
    n = len(masks)
    held = [pltpu.VMEM(data[0].shape, F32)] * 4
    return pl.pallas_call(
        functools.partial(early_kernel, plan, masks, len(outputs)),
        in_specs=[SMEM] + [VMEM] * (2 * n + 4) + [ANY] * len(outputs),
        out_specs=[VMEM] * 4 + [ANY] * 2,
        out_shape=held + [jax.ShapeDtypeStruct(shape, F32)] * 2,
        input_output_aliases={1 + 2 * n + i: i for i in range(4 + len(outputs))},
        scratch_shapes=scratch(plan, n * plan.col_units) + [pltpu.SemaphoreType.DMA(())],
        compiler_params=pltpu.CompilerParams(vmem_limit_bytes=8 * MIB),
    )(meta, *gathered, *swapped, *held_in_vmem(data), *in_hbm(outputs))


def late(plan, masks, meta, gathered, swapped, lefts, data, outputs):
    n, w = len(masks), plan.width
    first = 1 + 2 * n + len(lefts)
    held = [pltpu.VMEM(data[0].shape, F32)] * 4
    shape = jax.ShapeDtypeStruct(outputs[0].shape, F32)
    return pl.pallas_call(
        functools.partial(late_kernel, plan, masks),
        in_specs=[SMEM] + [VMEM] * (2 * n + len(lefts) + 4) + [ANY] * 2,
        out_specs=[VMEM] * 4 + [ANY] * 4,
        out_shape=held + [shape] * 4,
        input_output_aliases={first + i: i for i in range(6)},
        scratch_shapes=scratch(plan, n * plan.col_units)
        + [pltpu.VMEM((plan.row_blocks, 2 * w, w), BF16)]
        + [pltpu.SemaphoreType.DMA(())],
        compiler_params=pltpu.CompilerParams(vmem_limit_bytes=8 * MIB),
        name="late",
    )(meta, *gathered, *swapped, *lefts, *held_in_vmem(data), *in_hbm(outputs))[4:]


def flat(x):
    a, q, b, m = x.shape
    return x.reshape(a, q, b, m // LANES, LANES).transpose(0, 1, 3, 2, 4).reshape(a, q, m // LANES, b, 1, LANES)


def unflat(y, shape):
    a, q, b, m = shape
    return y.reshape(a, q, m // LANES, b, LANES).transpose(0, 1, 3, 2, 4).reshape(shape)


def shards(upper_s, upper_t, left_vectors, right_vectors, window_starts, selection, window_factors):
    rows, cols = lax.axis_size("row"), lax.axis_size("col")
    shape = upper_s.shape
    plan = Plan(rows, cols, shape[0], shape[2], window_starts.shape[0], window_factors.shape[1], shape[1])
    meta = jnp.stack([lax.axis_index("row"), lax.axis_index("col")]).astype(jnp.int32)
    numbers = jnp.arange(plan.blocks, dtype=jnp.int32)
    windows = jnp.arange(window_starts.shape[1], dtype=jnp.int32)
    same = window_starts[:, None, :] == numbers[None, :, None]
    inv = jnp.sum(jnp.where(same, windows + 1, 0), axis=2) - 1
    over = plan.overflows(window_starts)

    inputs = [flat(x) for x in (upper_s, upper_t, left_vectors, right_vectors)]
    return steps(plan, meta, inv, over, inputs, shape, selection, window_factors)


def steps(plan, meta, inv, over, inputs, shape, selection, window_factors):
    cols = plan.cols
    held = stage(plan, inputs[:2]) + stage(plan, inputs[2:])
    window_factors = window_factors.reshape((-1,) + window_factors.shape[3:])
    sources = [window_factors, lax.ppermute(window_factors, "row", plan.swap())]
    for t in range(plan.stages):
        first, rest = pack(plan, t, route(plan, t, meta, inv), sources)
        sent = functools.partial(lax.ppermute, axis_name="row", perm=plan.turn(t))
        moved = sent(first)
        sources += [moved, lax.cond(over[t], sent, lambda x: x, rest)]
    jobs = route(plan, plan.stages, meta, inv)
    moves = orders(plan, jobs, selection)
    made, left = compose(plan, jobs, moves, sources)

    lefts = [left]
    for shift in range(1, cols):
        lefts.append(lax.ppermute(left, "col", [(c, (c + shift) % cols) for c in range(cols)]))
    gathered = [made]
    swapped = [lax.ppermute(made, "row", plan.swap())]
    for t in range(plan.stages):
        gathered += [lax.ppermute(x, "row", plan.turn(t)) for x in gathered]
    swapped += [lax.ppermute(x, "row", plan.swap()) for x in gathered[1:]]
    last = (1 << plan.stages) - 1
    outputs = []
    for masks in ([0], list(range(1, last))):
        made = [gathered[m] for m in masks], [swapped[m] for m in masks]
        done = early(plan, masks, meta, *made, held, inputs[0].shape, outputs)
        held, outputs = done[:4], done[4:]
    done = late(plan, [last], meta, gathered[last:], swapped[last:], lefts, held, outputs)
    return tuple(unflat(x, shape) for x in (done[2], done[3], done[0], done[1]))


def solution(mesh):
    spread = P(None, "row", None, "col")
    return jax.shard_map(
        shards,
        mesh=mesh,
        in_specs=(spread,) * 4 + (P(), P(), P(None, "row", None, None, None)),
        out_specs=(spread,) * 4,
        check_vma=False,
    )
```

profile of v0, /device:TPU:0, one launch (start us, length us, event | category | flops | bytes accessed | tf_op | source)
XLA Modules:
  0.0 175.2 jit_solution(16965987388210567073)
XLA Ops:
  0.6 0.6 collective-permute-start.2
  1.2 0.1 pad_add_fusion.meta
  1.3 0.8 select_reduce_fusion
  2.0 2.9 %shard_map.166.jobs = s32[19]{0:T(128)S(1)} custom-call(s32[2]{0:T(128)S(1)} %pad_add_fusion.meta, s32[3,32]{1,0:T(4,128)S(1)} %broadcast_add_fusion.inv), custom_call_target="tpu_custom_call" | custom-call | tf_op jit(solution)/shard_map/pallas_call | solution.py:187
  4.9 1.9 %collective-permute-done.2.refs_1_ = f32[12,256,256]{2,1,0:T(8,128)} collective-permute-done((f32[12,256,256]{2,1,0:T(8,128)}, f32[12,256,256]{2,1,0:T(8,128)}, u32[]{:S(2)}, u32[]{:S(2)}) %collective-permute-start.2) | collective-permute-done | bytes 3145760 | tf_op jit(solution)/shard_map/ppermute | solution.py:577
  6.8 2.7 %shard_map.167 = (f32[6,256,256]{2,1,0:T(8,128)}, f32[12,256,256]{2,1,0:T(8,128)}) custom-call(s32[19]{0:T(128)S(1)} %shard_map.166.jobs, f32[12,256,256]{2,1,0:T(8,128)} %bitcast.48, f32[12,256,256]{2,1,0:T(8,128)} %collective-permute-done.2.refs_1_), custom_call_target="tpu_custom_call" | custom-call | tf_op jit(solution)/shard_map/pallas_call | solution.py:237
  9.5 2.9 %collective-permute-start.3 = (f32[6,256,256]{2,1,0:T(8,128)}, f32[6,256,256]{2,1,0:T(8,128)S(1)}, u32[]{:S(2)}, u32[]{:S(2)}) collective-permute-start(f32[6,256,256]{2,1,0:T(8,128)} %get-tuple-element.40), channel_id=1, source_target_pairs={{0,8},{4,20},{8,0},{12,28},{16,24},{20,4},{24,16},{28,12},{1,9},{5... | collective-permute-start | bytes 4718600 | tf_op jit(solution)/shard_map/ppermute | solution.py:581
  12.5 0.8 reshape.350
  13.2 4.8 %shard_map.168.jobs = s32[10]{0:T(128)S(1)} custom-call(s32[2]{0:T(128)S(1)} %pad_add_fusion.meta, s32[3,32]{1,0:T(4,128)S(1)} %broadcast_add_fusion.inv), custom_call_target="tpu_custom_call" | custom-call | tf_op jit(solution)/shard_map/pallas_call | solution.py:187
  18.0 0.1 xor.22
  18.2 0.9 add_reduce_fusion
  19.0 0.1 reshape.351
  19.1 0.1 reduce_max.9
  19.2 0.6 fusion.10
  20.5 0.0 copy-start
  20.5 45.9 %conditional.2 = (f32[12,256,256]{2,1,0:T(8,128)}) conditional(s32[]{:T(128)} %bitcast.3, f32[12,256,256]{2,1,0:T(8,128)} %get-tuple-element.41, f32[12,256,256]{2,1,0:T(8,128)} %get-tuple-element.41), branch_computations={%region_3.4_spmd, %region_4.5_spmd} | conditional | bytes 18874416 | solution.py:582
  20.5 0.1 collective-permute-start
  20.6 44.2 %collective-permute-done = f32[12,256,256]{2,1,0:T(8,128)S(1)} collective-permute-done((f32[12,256,256]{2,1,0:T(8,128)}, f32[12,256,256]{2,1,0:T(8,128)S(1)}, u32[]{:S(2)}, u32[]{:S(2)}) %collective-permute-start) | collective-permute-done | bytes 3145760 | tf_op jit(solution)/shard_map/cond/branch_1_fun/ppermute | solution.py:582
  64.8 1.7 copy.35
  66.4 1.8 %shard_map.169 = (f32[6,256,256]{2,1,0:T(8,128)}, f32[3,256,256]{2,1,0:T(8,128)}) custom-call(s32[10]{0:T(128)S(1)} %shard_map.168.jobs, f32[12,256,256]{2,1,0:T(8,128)} %bitcast.49, f32[12,256,256]{2,1,0:T(8,128)} %collective-permute-done.2.refs_1_, f32[6,256,256]{2,1,0:T(8,128)S(1)} %collective-permute-done.3.refs_2_, ...), custom_call_target="tpu_custom_call" | custom-call | tf_op jit(solution)/shard_map/pallas_call | solution.py:237
  68.2 4.6 %collective-permute-start.4 = (f32[6,256,256]{2,1,0:T(8,128)}, f32[6,256,256]{2,1,0:T(8,128)}, u32[]{:S(2)}, u32[]{:S(2)}) collective-permute-start(f32[6,256,256]{2,1,0:T(8,128)} %get-tuple-element.42), channel_id=1, source_target_pairs={{0,16},{4,12},{8,24},{12,4},{16,0},{20,28},{24,8},{28,20},{1,17},{... | collective-permute-start | bytes 4718600 | tf_op jit(solution)/shard_map/ppermute | solution.py:581
  72.8 4.6 %shard_map.165.jobs = s32[18]{0:T(128)S(1)} custom-call(s32[2]{0:T(128)S(1)} %pad_add_fusion.meta, s32[3,32]{1,0:T(4,128)S(1)} %broadcast_add_fusion.inv), custom_call_target="tpu_custom_call" | custom-call | tf_op jit(solution)/shard_map/pallas_call | solution.py:187
  78.1 2.2 %orders.1.moves = bf16[9,256,256]{2,1,0:T(8,128)(2,1)S(1)} custom-call(s32[18]{0:T(128)S(1)} %shard_map.165.jobs, s32[3,16,256]{2,1,0:T(8,128)S(1)} %copy-done), custom_call_target="tpu_custom_call" | custom-call | tf_op jit(solution)/shard_map/orders/pallas_call | solution.py:275
  80.3 11.2 %collective-permute-done.4.refs_4_ = f32[6,256,256]{2,1,0:T(8,128)} collective-permute-done((f32[6,256,256]{2,1,0:T(8,128)}, f32[6,256,256]{2,1,0:T(8,128)}, u32[]{:S(2)}, u32[]{:S(2)}) %collective-permute-start.4) | collective-permute-done | bytes 1572896 | tf_op jit(solution)/shard_map/ppermute | solution.py:581
  91.5 4.3 %compose.1 = (f32[2,256,256]{2,1,0:T(8,128)S(1)}, f32[1,256,256]{2,1,0:T(8,128)S(1)}) custom-call(s32[18]{0:T(128)S(1)} %shard_map.165.jobs, bf16[9,256,256]{2,1,0:T(8,128)(2,1)S(1)} %orders.1.moves, f32[12,256,256]{2,1,0:T(8,128)} %bitcast.50, f32[12,256,256]{2,1,0:T(8,128)} %collective-permute-done.2.refs_1_, ...), custom_call_target="tpu_custom_call" | custom-call | tf_op jit(solution)/shard_map/compose/pallas_call | solution.py:329
  95.8 3.0 %collective-permute-start.5 = (f32[2,256,256]{2,1,0:T(8,128)S(1)}, f32[2,256,256]{2,1,0:T(8,128)S(1)}, u32[]{:S(2)}, u32[]{:S(2)}) collective-permute-start(f32[2,256,256]{2,1,0:T(8,128)S(1)} %get-tuple-element.44.refs_0_), channel_id=1, source_target_pairs={{0,8},{4,20},{8,0},{12,28},{16,24},{20,4},{24,16},{28,12},{1,9},{5... | collective-permute-start | bytes 1572872 | tf_op jit(solution)/shard_map/ppermute | solution.py:593
  98.9 1.4 collective-permute-start.11
  100.2 11.4 %collective-permute-done.5.refs_0_ = f32[2,256,256]{2,1,0:T(8,128)S(1)} collective-permute-done((f32[2,256,256]{2,1,0:T(8,128)S(1)}, f32[2,256,256]{2,1,0:T(8,128)S(1)}, u32[]{:S(2)}, u32[]{:S(2)}) %collective-permute-start.5) | collective-permute-done | bytes 524320 | tf_op jit(solution)/shard_map/ppermute | solution.py:593
  111.6 0.3 collective-permute-start.6
  111.9 0.0 collective-permute-start.14
  111.9 0.0 collective-permute-done.11.refs_1_
  111.9 0.5 collective-permute-start.13
  112.4 0.0 collective-permute-start.12
  112.4 8.4 %collective-permute-done.6.refs_0_ = f32[2,256,256]{2,1,0:T(8,128)S(1)} collective-permute-done((f32[2,256,256]{2,1,0:T(8,128)S(1)}, f32[2,256,256]{2,1,0:T(8,128)S(1)}, u32[]{:S(2)}, u32[]{:S(2)}) %collective-permute-start.6) | collective-permute-done | bytes 524320 | tf_op jit(solution)/shard_map/ppermute | solution.py:593
  120.8 0.0 collective-permute-start.7
  120.8 1.4 collective-permute-start.10
  122.2 0.0 collective-permute-done.14.refs_1_
  122.2 0.0 collective-permute-start.9
  122.2 0.0 collective-permute-done.13.refs_3_
  122.2 1.0 collective-permute-start.8
  123.2 8.1 %shard_map.170 = (f32[4,8,256,256]{3,2,1,0:T(8,128)S(1)}, f32[4,8,256,256]{3,2,1,0:T(8,128)S(1)}) custom-call(f32[4,256,2,8,1,128]{5,4,3,2,1,0:T(1,128)} %bitcast.51, f32[4,256,2,8,1,128]{5,4,3,2,1,0:T(1,128)} %bitcast.52), custom_call_target="tpu_custom_call" | custom-call | tf_op jit(solution)/shard_map/pallas_call | solution.py:381
  131.3 8.1 %shard_map.171 = (f32[4,8,256,256]{3,2,1,0:T(8,128)S(1)}, f32[4,8,256,256]{3,2,1,0:T(8,128)S(1)}) custom-call(f32[4,256,2,8,1,128]{5,4,3,2,1,0:T(1,128)} %bitcast.53, f32[4,256,2,8,1,128]{5,4,3,2,1,0:T(1,128)} %bitcast.54), custom_call_target="tpu_custom_call" | custom-call | tf_op jit(solution)/shard_map/pallas_call | solution.py:381
  139.4 5.8 %shard_map.172 = (f32[4,8,256,256]{3,2,1,0:T(8,128)S(1)}, f32[4,8,256,256]{3,2,1,0:T(8,128)S(1)}, f32[4,8,256,256]{3,2,1,0:T(8,128)S(1)}, f32[4,8,256,256]{3,2,1...) custom-call(s32[2]{0:T(128)S(1)} %pad_add_fusion.meta, ...), custom_call_target="tpu_custom_call", output_to_operand_aliasing={{0}: (3, {}), {1}: (4, {}), {2}: (5, {}), {3}: (6, {})} | custom-call | tf_op jit(solution)/shard_map/pallas_call | solution.py:518
  145.2 0.0 collective-permute-done.12.refs_2_
  145.3 11.1 %shard_map.173 = (f32[4,8,256,256]{3,2,1,0:T(8,128)S(1)}, f32[4,8,256,256]{3,2,1,0:T(8,128)S(1)}, f32[4,8,256,256]{3,2,1,0:T(8,128)S(1)}, f32[4,8,256,256]{3,2,1...) custom-call(s32[2]{0:T(128)S(1)} %pad_add_fusion.meta, ...), custom_call_target="tpu_custom_call", output_to_operand_aliasing={{0}: (5, {}), {1}: (6, {}), {2}: (7, {}), {3}: (8, {}), {4}... | custom-call | tf_op jit(solution)/shard_map/pallas_call | solution.py:518
  156.3 0.0 collective-permute-done.10.refs_5_
  156.3 0.0 collective-permute-done.9.refs_4_
  156.4 18.9 %late.1 = (f32[4,8,256,256]{3,2,1,0:T(8,128)S(1)}, f32[4,8,256,256]{3,2,1,0:T(8,128)S(1)}, f32[4,8,256,256]{3,2,1,0:T(8,128)S(1)}, f32[4,8,256,256]{3,2,1,0:T(8,...) custom-call(s32[2]{0:T(128)S(1)} %pad_add_fusion.meta, ...), custom_call_target="tpu_custom_call", output_to_operand_aliasing={{0}: (7, {}), {1}: (8, {}), {2}: (9, {}), {3}: (10, {}), {4... | custom-call | tf_op jit(solution)/shard_map/late/pallas_call | solution.py:534
  (12 shorter events, 0.1 us)
Async XLA Ops:
  0.6 6.2 %collective-permute-start.2 = (f32[12,256,256]{2,1,0:T(8,128)}, f32[12,256,256]{2,1,0:T(8,128)}, u32[]{:S(2)}, u32[]{:S(2)}) collective-permute-start(f32[12,256,256]{2,1,0:T(8,128)} %bitcast.47), channel_id=1, source_target_pairs={{0,4},{4,0},{8,12},{12,8},{16,20},{20,16},{24,28},{28,24},{1,5},{5... | collective-permute-start | bytes 9437192 | tf_op jit(solution)/shard_map/ppermute | solution.py:577
  9.5 56.9 %collective-permute-start.3 = (f32[6,256,256]{2,1,0:T(8,128)}, f32[6,256,256]{2,1,0:T(8,128)S(1)}, u32[]{:S(2)}, u32[]{:S(2)}) collective-permute-start(f32[6,256,256]{2,1,0:T(8,128)} %get-tuple-element.40), channel_id=1, source_target_pairs={{0,8},{4,20},{8,0},{12,28},{16,24},{20,4},{24,16},{28,12},{1,9},{5... | collective-permute-start | bytes 4718600 | tf_op jit(solution)/shard_map/ppermute | solution.py:581
  20.5 57.6 %copy-start = (s32[3,16,256]{2,1,0:T(8,128)S(1)}, s32[3,16,256]{2,1,0:T(8,128)}, u32[]{:S(2)}) copy-start(s32[3,16,256]{2,1,0:T(8,128)} %flags.1) | copy-start | bytes 147460
  20.5 44.3 %collective-permute-start = (f32[12,256,256]{2,1,0:T(8,128)}, f32[12,256,256]{2,1,0:T(8,128)S(1)}, u32[]{:S(2)}, u32[]{:S(2)}) collective-permute-start(f32[12,256,256]{2,1,0:T(8,128)} %param.1), channel_id=1, source_target_pairs={{0,8},{4,20},{8,0},{12,28},{16,24},{20,4},{24,16},{28,12},{1,9},{5... | collective-permute-start | bytes 9437192 | tf_op jit(solution)/shard_map/cond/branch_1_fun/ppermute | solution.py:582
  68.2 23.3 %collective-permute-start.4 = (f32[6,256,256]{2,1,0:T(8,128)}, f32[6,256,256]{2,1,0:T(8,128)}, u32[]{:S(2)}, u32[]{:S(2)}) collective-permute-start(f32[6,256,256]{2,1,0:T(8,128)} %get-tuple-element.42), channel_id=1, source_target_pairs={{0,16},{4,12},{8,24},{12,4},{16,0},{20,28},{24,8},{28,20},{1,17},{... | collective-permute-start | bytes 4718600 | tf_op jit(solution)/shard_map/ppermute | solution.py:581
  95.8 15.8 %collective-permute-start.5 = (f32[2,256,256]{2,1,0:T(8,128)S(1)}, f32[2,256,256]{2,1,0:T(8,128)S(1)}, u32[]{:S(2)}, u32[]{:S(2)}) collective-permute-start(f32[2,256,256]{2,1,0:T(8,128)S(1)} %get-tuple-element.44.refs_0_), channel_id=1, source_target_pairs={{0,8},{4,20},{8,0},{12,28},{16,24},{20,4},{24,16},{28,12},{1,9},{5... | collective-permute-start | bytes 1572872 | tf_op jit(solution)/shard_map/ppermute | solution.py:593
  98.9 13.0 %collective-permute-start.11 = (f32[2,256,256]{2,1,0:T(8,128)S(1)}, f32[2,256,256]{2,1,0:T(8,128)S(1)}, u32[]{:S(2)}, u32[]{:S(2)}) collective-permute-start(f32[2,256,256]{2,1,0:T(8,128)S(1)} %get-tuple-element.44.refs_0_), channel_id=1, source_target_pairs={{0,16},{4,12},{8,24},{12,4},{16,0},{20,28},{24,8},{28,20},{1,17},{... | collective-permute-start | bytes 1572872 | tf_op jit(solution)/shard_map/ppermute | solution.py:593
  111.6 9.2 %collective-permute-start.6 = (f32[2,256,256]{2,1,0:T(8,128)S(1)}, f32[2,256,256]{2,1,0:T(8,128)S(1)}, u32[]{:S(2)}, u32[]{:S(2)}) collective-permute-start(f32[2,256,256]{2,1,0:T(8,128)S(1)} %collective-permute-done.5.refs_0_), channel_id=1, source_target_pairs={{0,16},{4,12},{8,24},{12,4},{16,0},{20,28},{24,8},{28,20},{1,17},{... | collective-permute-start | bytes 1572872 | tf_op jit(solution)/shard_map/ppermute | solution.py:593
  111.9 10.3 %collective-permute-start.14 = (f32[2,256,256]{2,1,0:T(8,128)S(1)}, f32[2,256,256]{2,1,0:T(8,128)S(1)}, u32[]{:S(2)}, u32[]{:S(2)}) collective-permute-start(f32[2,256,256]{2,1,0:T(8,128)S(1)} %get-tuple-element.44.refs_0_), channel_id=1, source_target_pairs={{0,4},{4,0},{8,12},{12,8},{16,20},{20,16},{24,28},{28,24},{1,5},{5... | collective-permute-start | bytes 1572872 | tf_op jit(solution)/shard_map/ppermute | solution.py:591
  111.9 10.3 %collective-permute-start.13 = (f32[2,256,256]{2,1,0:T(8,128)S(1)}, f32[2,256,256]{2,1,0:T(8,128)S(1)}, u32[]{:S(2)}, u32[]{:S(2)}) collective-permute-start(f32[2,256,256]{2,1,0:T(8,128)S(1)} %collective-permute-done.11.refs_1_), channel_id=1, source_target_pairs={{0,4},{4,0},{8,12},{12,8},{16,20},{20,16},{24,28},{28,24},{1,5},{5... | collective-permute-start | bytes 1572872 | tf_op jit(solution)/shard_map/ppermute | solution.py:594
  112.4 32.8 %collective-permute-start.12 = (f32[2,256,256]{2,1,0:T(8,128)S(1)}, f32[2,256,256]{2,1,0:T(8,128)S(1)}, u32[]{:S(2)}, u32[]{:S(2)}) collective-permute-start(f32[2,256,256]{2,1,0:T(8,128)S(1)} %collective-permute-done.5.refs_0_), channel_id=1, source_target_pairs={{0,4},{4,0},{8,12},{12,8},{16,20},{20,16},{24,28},{28,24},{1,5},{5... | collective-permute-start | bytes 1572872 | tf_op jit(solution)/shard_map/ppermute | solution.py:594
  120.8 35.5 %collective-permute-start.7 = (f32[2,256,256]{2,1,0:T(8,128)S(1)}, f32[2,256,256]{2,1,0:T(8,128)S(1)}, u32[]{:S(2)}, u32[]{:S(2)}) collective-permute-start(f32[2,256,256]{2,1,0:T(8,128)S(1)} %collective-permute-done.6.refs_0_), channel_id=1, source_target_pairs={{0,4},{4,0},{8,12},{12,8},{16,20},{20,16},{24,28},{28,24},{1,5},{5... | collective-permute-start | bytes 1572872 | tf_op jit(solution)/shard_map/ppermute | solution.py:594
  120.8 35.5 %collective-permute-start.10 = (f32[1,256,256]{2,1,0:T(8,128)S(1)}, f32[1,256,256]{2,1,0:T(8,128)S(1)}, u32[]{:S(2)}, u32[]{:S(2)}) collective-permute-start(f32[1,256,256]{2,1,0:T(8,128)S(1)} %get-tuple-element.45.refs_2_), channel_id=1, source_target_pairs={{0,3},{1,0},{2,1},{3,2},{4,7},{5,4},{6,5},{7,6},{8,11},{9,8},{10,9... | collective-permute-start | bytes 786440 | tf_op jit(solution)/shard_map/ppermute | solution.py:589
  122.2 34.1 %collective-permute-start.9 = (f32[1,256,256]{2,1,0:T(8,128)S(1)}, f32[1,256,256]{2,1,0:T(8,128)S(1)}, u32[]{:S(2)}, u32[]{:S(2)}) collective-permute-start(f32[1,256,256]{2,1,0:T(8,128)S(1)} %get-tuple-element.45.refs_2_), channel_id=1, source_target_pairs={{0,2},{1,3},{2,0},{3,1},{4,6},{5,7},{6,4},{7,5},{8,10},{9,11},{10,... | collective-permute-start | bytes 786440 | tf_op jit(solution)/shard_map/ppermute | solution.py:589
  122.2 34.1 %collective-permute-start.8 = (f32[1,256,256]{2,1,0:T(8,128)S(1)}, f32[1,256,256]{2,1,0:T(8,128)S(1)}, u32[]{:S(2)}, u32[]{:S(2)}) collective-permute-start(f32[1,256,256]{2,1,0:T(8,128)S(1)} %get-tuple-element.45.refs_2_), channel_id=1, source_target_pairs={{0,1},{1,2},{2,3},{3,0},{4,5},{5,6},{6,7},{7,4},{8,9},{9,10},{10,1... | collective-permute-start | bytes 786440 | tf_op jit(solution)/shard_map/ppermute | solution.py:589
where the time goes:
time: 175 us
  waiting for transfers between devices  77.1 us (44%)
  Pallas kernels  75.3 us (43%)
  starting transfers between devices  15.6 us (9%)
  local copies, waits for them, and re-layouts  3.19 us (2%)
  between operations  2.14 us (1%)
  other arithmetic  1.87 us (1%)
    ppermute x1, waiting for transfers between devices, steps(): sources += [moved, lax.cond(over[t], sent, lambda x: x, rest)]  44.2 us
    ppermute x3, waiting for transfers between devices, steps(): gathered += [lax.ppermute(x, 'row', plan.turn(t)) for x in gathered]  19.8 us
    pallas_call x1, Pallas kernels, late(): pl.pallas_call(functools.partial(late_kernel, plan, masks), in_specs=[SME...  18.9 us
    pallas_call x2, Pallas kernels, early(): pl.pallas_call(functools.partial(early_kernel, plan, masks, len(outputs))...  16.9 us
    pallas_call x2, Pallas kernels, stage(): pl.pallas_call(functools.partial(stage_kernel, plan, count), in_specs=[AN...  16.2 us
    pallas_call x3, Pallas kernels, route(): pl.pallas_call(functools.partial(route_kernel, plan, t), in_specs=[SMEM,...  12.3 us
    ppermute x2, waiting for transfers between devices, steps(): moved = sent(first)  11.2 us
    ppermute x2, starting transfers between devices, steps(): moved = sent(first)  7.47 us
  transfers between devices with their start and end apart: 14, of which 5 were waited for; matrix products, arithmetic and copies ran while one was open for 3% of the time, Pallas kernels for 27%

commit v1 on v0

--- a/solution.py
+++ b/solution.py
@@ -321,7 +321,7 @@
     for unit in range(plan.col_units):
         cols[unit] = held[unit]
     for unit in range(plan.row_units):
-        lefts[unit] = held[plan.col_units + unit]
+        lefts[unit] = held[plan.col_units + unit].T
 
 
 def compose(plan, jobs, moves, sources):
@@ -345,14 +345,13 @@
 
 
 def tiles(plan, act):
-    count = plan.row_blocks * plan.col_blocks * plan.parts
-
-    def step(index, carry):
-        a, rest = index // (plan.col_blocks * plan.parts), index % (plan.col_blocks * plan.parts)
-        act(a, rest // plan.parts, rest % plan.parts)
-        return carry
-
-    lax.fori_loop(0, count, step, 0)
+    def step(a, carry):
+        for b in range(plan.col_blocks):
+            for p in range(plan.parts):
+                act(a, b, p)
+        return carry
+
+    lax.fori_loop(0, plan.row_blocks, step, 0)
 
 
 def hbm_piece(ref, a, b, p):
@@ -360,32 +359,64 @@
 
 
 def vmem_piece(ref, a, b, p):
-    return ref.at[a, b, :, pl.ds(pl.multiple_of(p * LANES, LANES), LANES)]
-
-
-def stage_kernel(plan, count, *refs):
-    inputs, held, sems = refs[:count], refs[count : 2 * count], refs[2 * count]
-    for start in (True, False):
+    return ref.at[a, b, :, pl.ds(p * LANES, LANES)]
+
+
+def stage_kernel(plan, count, meta, *refs):
+    inputs, held, rest = refs[:count], refs[count : 2 * count], refs[2 * count :]
+    heights, sems = (rest[0], rest[1]) if len(rest) == 2 else (None, rest[0])
+
+    def copy(m, a, b, p):
+        sem = sems.at[m, a, b] if heights is not None else sems.at[m]
+        return pltpu.make_async_copy(hbm_piece(inputs[m], a, b, p), vmem_piece(held[m], a, b, p), sem)
+
+    for m in range(count):
+        tiles(plan, lambda a, b, p, m=m: copy(m, a, b, p).start())
+    if heights is None:
         for m in range(count):
-
-            def act(a, b, p, m=m):
-                copy = pltpu.make_async_copy(hbm_piece(inputs[m], a, b, p), vmem_piece(held[m], a, b, p), sems.at[m])
-                copy.start() if start else copy.wait()
-
-            tiles(plan, act)
-
-
-def stage(plan, inputs):
+            tiles(plan, lambda a, b, p, m=m: copy(m, a, b, p).wait())
+        return
+    for b in range(plan.col_blocks):
+        heights[b] = 0
+
+    def look(a, carry):
+        for b in range(plan.col_blocks):
+            for m in range(count):
+                for p in range(plan.parts):
+                    copy(m, a, b, p).wait()
+            below = a * plan.rows + meta[0] > b * plan.cols + meta[1]
+
+            @pl.when(jnp.logical_not(below))
+            def _(b=b):
+                heights[b] = a + 1
+
+            @pl.when(below)
+            def _(b=b):
+                top = jnp.abs(held[0][a, b])
+                for m in range(1, count):
+                    top = jnp.maximum(top, jnp.abs(held[m][a, b]))
+
+                @pl.when(jnp.max(top) > 0.0)
+                def _():
+                    heights[b] = a + 1
+
+        return carry
+
+    lax.fori_loop(0, plan.row_blocks, look, 0)
+
+
+def stage(plan, meta, inputs, heights):
     shape = (plan.row_blocks, plan.col_blocks, plan.width, plan.width)
     count = len(inputs)
+    extra = [jax.ShapeDtypeStruct((plan.col_blocks,), jnp.int32)] if heights else []
     return pl.pallas_call(
         functools.partial(stage_kernel, plan, count),
-        in_specs=[ANY] * count,
-        out_specs=[VMEM] * count,
-        out_shape=[pltpu.VMEM(shape, F32)] * count,
-        scratch_shapes=[pltpu.SemaphoreType.DMA((count,))],
+        in_specs=[SMEM] + [ANY] * count,
+        out_specs=[VMEM] * count + [SMEM] * len(extra),
+        out_shape=[pltpu.VMEM(shape, F32)] * count + extra,
+        scratch_shapes=[pltpu.SemaphoreType.DMA((count,) + (shape[:2] if heights else ()))],
         compiler_params=pltpu.CompilerParams(vmem_limit_bytes=MIB),
-    )(*in_hbm(inputs))
+    )(meta, *in_hbm(inputs))
 
 
 def combine(plan, m, core):
@@ -397,23 +428,30 @@
 
 
 def write_out(plan, source, target, b, sem):
-    def step(index, carry):
-        a, p = index // plan.parts, index % plan.parts
-        pltpu.make_async_copy(vmem_piece(source, a, b, p), hbm_piece(target, a, b, p), sem).start()
-        return carry
-
-    lax.fori_loop(0, plan.row_blocks * plan.parts, step, 0)
+    for a in range(plan.row_blocks):
+        for p in range(plan.parts):
+            pltpu.make_async_copy(vmem_piece(source, a, b, p), hbm_piece(target, a, b, p), sem).start()
 
 
 def settle_out(plan, source, target, count, sem):
     def step(index, carry):
-        pltpu.make_async_copy(vmem_piece(source, 0, 0, 0), hbm_piece(target, 0, 0, 0), sem).wait()
-        return carry
-
-    lax.fori_loop(0, count * plan.row_blocks * plan.parts, step, 0)
-
-
-def columns(plan, masks, meta, gathered, swapped, data, outputs, high, low, places, sem):
+        for a in range(plan.row_blocks):
+            for p in range(plan.parts):
+                pltpu.make_async_copy(vmem_piece(source, a, 0, p), hbm_piece(target, a, 0, p), sem).wait()
+        return carry
+
+    lax.fori_loop(0, count, step, 0)
+
+
+def by_height(plan, height, act):
+    for count in range(1, plan.row_blocks + 1):
+
+        @pl.when(height == count)
+        def _(count=count):
+            act(count)
+
+
+def columns(plan, masks, meta, heights, gathered, swapped, data, outputs, high, low, places, sem):
     core, here = meta[0] % 2, meta[0] // 2
     count = jnp.int32(0)
     slots = {}
@@ -437,27 +475,33 @@
 
     def step(index, carry):
         b = places[index]
-        for m, kind in ((2, 0), (3, 1), (0, 1), (1, 1)):
+        for m, kind in ((2, 0), (3, 1)):
             ref = data[m]
             for a in range(plan.row_blocks):
                 ref[a, b] = product(halves(ref[a, b]), (high[kind, b], low[kind, b]))
-            if m >= 2:
-                write_out(plan, ref, outputs[m - 2], b, sem)
+            write_out(plan, ref, outputs[m - 2], b, sem)
+
+        def pencil(height):
+            for a in range(height):
+                for m in range(2):
+                    data[m][a, b] = product(halves(data[m][a, b]), (high[1, b], low[1, b]))
+
+        by_height(plan, heights[b], pencil)
         return carry
 
     lax.fori_loop(0, count, step, 0)
     return count
 
 
-def early_kernel(plan, masks, extra, meta, *refs):
+def early_kernel(plan, masks, extra, meta, heights, *refs):
     n = len(masks)
     gathered, swapped, refs = refs[:n], refs[n : 2 * n], refs[2 * n + 4 + extra :]
     data, outputs, (high, low, places, sem) = refs[:4], refs[4:6], refs[6:]
-    count = columns(plan, masks, meta, gathered, swapped, data, outputs, high, low, places, sem)
+    count = columns(plan, masks, meta, heights, gathered, swapped, data, outputs, high, low, places, sem)
     settle_out(plan, data[2], outputs[0], 2 * count, sem)
 
 
-def late_kernel(plan, masks, meta, *refs):
+def late_kernel(plan, masks, meta, heights, *refs):
     n, br = len(masks), plan.row_blocks
     gathered, swapped, refs = refs[:n], refs[n : 2 * n], refs[2 * n :]
     lefts, refs = refs[: plan.cols], refs[plan.cols + 6 :]
@@ -471,18 +515,22 @@
 
             @pl.when(place < br)
             def _(shift=shift, unit=unit, place=place):
-                h, l = halves(lefts[shift][unit].T)
+                h, l = halves(lefts[shift][unit])
                 left[place, pl.ds(0, plan.width)] = h
                 left[place, pl.ds(plan.width, plan.width)] = l
 
-    count = columns(plan, masks, meta, gathered, swapped, data, outputs[:2], high, low, places, sem)
+    count = columns(plan, masks, meta, heights, gathered, swapped, data, outputs[:2], high, low, places, sem)
 
     def rows(b, carry):
+        def pencil(height):
+            for a in range(height):
+                for m in range(2):
+                    y = halves(data[m][a, b])
+                    both = dot(left[a], y[0])
+                    data[m][a, b] = both[:w] + (both[w:] + dot(left[a, :w], y[1]))
+
+        by_height(plan, heights[b], pencil)
         for m in range(2):
-            for a in range(br):
-                y = halves(data[m][a, b])
-                both = dot(left[a], y[0])
-                data[m][a, b] = both[:w] + (both[w:] + dot(left[a, :w], y[1]))
             write_out(plan, data[m], outputs[2 + m], b, sem)
         return carry
 
@@ -512,28 +560,28 @@
     ]
 
 
-def early(plan, masks, meta, gathered, swapped, data, shape, outputs):
+def early(plan, masks, meta, heights, gathered, swapped, data, shape, outputs):
     n = len(masks)
     held = [pltpu.VMEM(data[0].shape, F32)] * 4
     return pl.pallas_call(
         functools.partial(early_kernel, plan, masks, len(outputs)),
-        in_specs=[SMEM] + [VMEM] * (2 * n + 4) + [ANY] * len(outputs),
+        in_specs=[SMEM, SMEM] + [VMEM] * (2 * n + 4) + [ANY] * len(outputs),
         out_specs=[VMEM] * 4 + [ANY] * 2,
         out_shape=held + [jax.ShapeDtypeStruct(shape, F32)] * 2,
-        input_output_aliases={1 + 2 * n + i: i for i in range(4 + len(outputs))},
+        input_output_aliases={2 + 2 * n + i: i for i in range(4 + len(outputs))},
         scratch_shapes=scratch(plan, n * plan.col_units) + [pltpu.SemaphoreType.DMA(())],
         compiler_params=pltpu.CompilerParams(vmem_limit_bytes=8 * MIB),
-    )(meta, *gathered, *swapped, *held_in_vmem(data), *in_hbm(outputs))
-
-
-def late(plan, masks, meta, gathered, swapped, lefts, data, outputs):
+    )(meta, heights, *gathered, *swapped, *held_in_vmem(data), *in_hbm(outputs))
+
+
+def late(plan, masks, meta, heights, gathered, swapped, lefts, data, outputs):
     n, w = len(masks), plan.width
-    first = 1 + 2 * n + len(lefts)
+    first = 2 + 2 * n + len(lefts)
     held = [pltpu.VMEM(data[0].shape, F32)] * 4
     shape = jax.ShapeDtypeStruct(outputs[0].shape, F32)
     return pl.pallas_call(
         functools.partial(late_kernel, plan, masks),
-        in_specs=[SMEM] + [VMEM] * (2 * n + len(lefts) + 4) + [ANY] * 2,
+        in_specs=[SMEM, SMEM] + [VMEM] * (2 * n + len(lefts) + 4) + [ANY] * 2,
         out_specs=[VMEM] * 4 + [ANY] * 4,
         out_shape=held + [shape] * 4,
         input_output_aliases={first + i: i for i in range(6)},
@@ -542,7 +590,7 @@
         + [pltpu.SemaphoreType.DMA(())],
         compiler_params=pltpu.CompilerParams(vmem_limit_bytes=8 * MIB),
         name="late",
-    )(meta, *gathered, *swapped, *lefts, *held_in_vmem(data), *in_hbm(outputs))[4:]
+    )(meta, heights, *gathered, *swapped, *lefts, *held_in_vmem(data), *in_hbm(outputs))[4:]
 
 
 def flat(x):
@@ -572,7 +620,8 @@
 
 def steps(plan, meta, inv, over, inputs, shape, selection, window_factors):
     cols = plan.cols
-    held = stage(plan, inputs[:2]) + stage(plan, inputs[2:])
+    *held, heights = stage(plan, meta, inputs[:2], True)
+    held = held + list(stage(plan, meta, inputs[2:], False))
     window_factors = window_factors.reshape((-1,) + window_factors.shape[3:])
     sources = [window_factors, lax.ppermute(window_factors, "row", plan.swap())]
     for t in range(plan.stages):
@@ -596,9 +645,9 @@
     outputs = []
     for masks in ([0], list(range(1, last))):
         made = [gathered[m] for m in masks], [swapped[m] for m in masks]
-        done = early(plan, masks, meta, *made, held, inputs[0].shape, outputs)
+        done = early(plan, masks, meta, heights, *made, held, inputs[0].shape, outputs)
         held, outputs = done[:4], done[4:]
-    done = late(plan, [last], meta, gathered[last:], swapped[last:], lefts, held, outputs)
+    done = late(plan, [last], meta, heights, gathered[last:], swapped[last:], lefts, held, outputs)
     return tuple(unflat(x, shape) for x in (done[2], done[3], done[0], done[1]))
 
 

time: 175 us -> 169 us (0.966)
  Pallas kernels: 75.3 us -> 68.2 us
    pallas_call x1, Pallas kernels: 18.9 us -> 13 us  [late(): pl.pallas_call(functools.partial(late_kernel, plan, masks), in_specs=[SME...]
    pallas_call x2, Pallas kernels: 16.9 us -> 13.2 us  [early(): pl.pallas_call(functools.partial(early_kernel, plan, masks, len(outputs))...]
    pallas_call x2, Pallas kernels: 16.2 us -> 18.6 us  [stage(): pl.pallas_call(functools.partial(stage_kernel, plan, count), in_specs=[SM...]
  transfers between devices with their start and end apart: 14 -> 14, of which waited for: 5 -> 5; matrix products, arithmetic and copies ran while one was open for 3% -> 3% of each run, Pallas kernels for 27% -> 28%
where the time goes in v1:
time: 169 us; the launch traced here: 168 us
  waiting for transfers between devices  77.2 us (46%)
  Pallas kernels  68.2 us (40%)
  starting transfers between devices  15.6 us (9%)
  local copies, waits for them, and re-layouts  3.19 us (2%)
  between operations  2.3 us (1%)
  other arithmetic  1.87 us (1%)
    ppermute x1, waiting for transfers between devices, steps(): sources += [moved, lax.cond(over[t], sent, lambda x: x, rest)]  44.2 us
    ppermute x3, waiting for transfers between devices, steps(): gathered += [lax.ppermute(x, 'row', plan.turn(t)) for x in gathered]  19.9 us
    pallas_call x2, Pallas kernels, stage(): pl.pallas_call(functools.partial(stage_kernel, plan, count), in_specs=[SM...  18.6 us
    pallas_call x2, Pallas kernels, early(): pl.pallas_call(functools.partial(early_kernel, plan, masks, len(outputs))...  13.2 us
    pallas_call x1, Pallas kernels, late(): pl.pallas_call(functools.partial(late_kernel, plan, masks), in_specs=[SME...  13 us
    pallas_call x3, Pallas kernels, route(): pl.pallas_call(functools.partial(route_kernel, plan, t), in_specs=[SMEM,...  12.3 us
    ppermute x2, waiting for transfers between devices, steps(): moved = sent(first)  11.2 us
    ppermute x2, starting transfers between devices, steps(): moved = sent(first)  7.47 us
  transfers between devices with their start and end apart: 14, of which 5 were waited for; matrix products, arithmetic and copies ran while one was open for 3% of the time, Pallas kernels for 28%

profile of v1, /device:TPU:0, one launch (start us, length us, event | category | flops | bytes accessed | tf_op | source)
XLA Modules:
  0.0 168.3 jit_solution(15783696910665678005)
XLA Ops:
  0.6 0.6 collective-permute-start.2
  1.2 0.1 pad_add_fusion.meta
  1.3 0.8 select_reduce_fusion
  2.0 2.9 %shard_map.167.jobs = s32[19]{0:T(128)S(1)} custom-call(s32[2]{0:T(128)S(1)} %pad_add_fusion.meta, s32[3,32]{1,0:T(4,128)S(1)} %broadcast_add_fusion.inv), custom_call_target="tpu_custom_call" | custom-call | tf_op jit(solution)/shard_map/pallas_call | solution.py:187
  4.9 1.9 %collective-permute-done.2.refs_1_ = f32[12,256,256]{2,1,0:T(8,128)} collective-permute-done((f32[12,256,256]{2,1,0:T(8,128)}, f32[12,256,256]{2,1,0:T(8,128)}, u32[]{:S(2)}, u32[]{:S(2)}) %collective-permute-start.2) | collective-permute-done | bytes 3145760 | tf_op jit(solution)/shard_map/ppermute | solution.py:626
  6.8 2.7 %shard_map.168 = (f32[6,256,256]{2,1,0:T(8,128)}, f32[12,256,256]{2,1,0:T(8,128)}) custom-call(s32[19]{0:T(128)S(1)} %shard_map.167.jobs, f32[12,256,256]{2,1,0:T(8,128)} %bitcast.48, f32[12,256,256]{2,1,0:T(8,128)} %collective-permute-done.2.refs_1_), custom_call_target="tpu_custom_call" | custom-call | tf_op jit(solution)/shard_map/pallas_call | solution.py:237
  9.5 2.9 %collective-permute-start.3 = (f32[6,256,256]{2,1,0:T(8,128)}, f32[6,256,256]{2,1,0:T(8,128)S(1)}, u32[]{:S(2)}, u32[]{:S(2)}) collective-permute-start(f32[6,256,256]{2,1,0:T(8,128)} %get-tuple-element.42), channel_id=1, source_target_pairs={{0,8},{4,20},{8,0},{12,28},{16,24},{20,4},{24,16},{28,12},{1,9},{5... | collective-permute-start | bytes 4718600 | tf_op jit(solution)/shard_map/ppermute | solution.py:630
  12.5 0.8 reshape.354
  13.2 4.8 %shard_map.169.jobs = s32[10]{0:T(128)S(1)} custom-call(s32[2]{0:T(128)S(1)} %pad_add_fusion.meta, s32[3,32]{1,0:T(4,128)S(1)} %broadcast_add_fusion.inv), custom_call_target="tpu_custom_call" | custom-call | tf_op jit(solution)/shard_map/pallas_call | solution.py:187
  18.0 0.1 xor.22
  18.2 0.9 add_reduce_fusion
  19.0 0.1 reshape.355
  19.1 0.1 reduce_max.9
  19.2 0.6 fusion.10
  20.5 0.0 copy-start
  20.5 45.9 %conditional.2 = (f32[12,256,256]{2,1,0:T(8,128)}) conditional(s32[]{:T(128)} %bitcast.9, f32[12,256,256]{2,1,0:T(8,128)} %get-tuple-element.43, f32[12,256,256]{2,1,0:T(8,128)} %get-tuple-element.43), branch_computations={%region_3.4_spmd, %region_4.5_spmd} | conditional | bytes 18874416 | solution.py:631
  20.5 0.1 collective-permute-start
  20.6 44.2 %collective-permute-done = f32[12,256,256]{2,1,0:T(8,128)S(1)} collective-permute-done((f32[12,256,256]{2,1,0:T(8,128)}, f32[12,256,256]{2,1,0:T(8,128)S(1)}, u32[]{:S(2)}, u32[]{:S(2)}) %collective-permute-start) | collective-permute-done | bytes 3145760 | tf_op jit(solution)/shard_map/cond/branch_1_fun/ppermute | solution.py:631
  64.8 1.7 copy.35
  66.4 0.0 collective-permute-done.3.refs_2_
  66.4 1.8 %shard_map.170 = (f32[6,256,256]{2,1,0:T(8,128)}, f32[3,256,256]{2,1,0:T(8,128)}) custom-call(s32[10]{0:T(128)S(1)} %shard_map.169.jobs, f32[12,256,256]{2,1,0:T(8,128)} %bitcast.49, f32[12,256,256]{2,1,0:T(8,128)} %collective-permute-done.2.refs_1_, f32[6,256,256]{2,1,0:T(8,128)S(1)} %collective-permute-done.3.refs_2_, ...), custom_call_target="tpu_custom_call" | custom-call | tf_op jit(solution)/shard_map/pallas_call | solution.py:237
  68.2 4.6 %collective-permute-start.4 = (f32[6,256,256]{2,1,0:T(8,128)}, f32[6,256,256]{2,1,0:T(8,128)}, u32[]{:S(2)}, u32[]{:S(2)}) collective-permute-start(f32[6,256,256]{2,1,0:T(8,128)} %get-tuple-element.44), channel_id=1, source_target_pairs={{0,16},{4,12},{8,24},{12,4},{16,0},{20,28},{24,8},{28,20},{1,17},{... | collective-permute-start | bytes 4718600 | tf_op jit(solution)/shard_map/ppermute | solution.py:630
  72.8 4.6 %shard_map.166.jobs = s32[18]{0:T(128)S(1)} custom-call(s32[2]{0:T(128)S(1)} %pad_add_fusion.meta, s32[3,32]{1,0:T(4,128)S(1)} %broadcast_add_fusion.inv), custom_call_target="tpu_custom_call" | custom-call | tf_op jit(solution)/shard_map/pallas_call | solution.py:187
  78.1 2.2 %orders.1.moves = bf16[9,256,256]{2,1,0:T(8,128)(2,1)S(1)} custom-call(s32[18]{0:T(128)S(1)} %shard_map.166.jobs, s32[3,16,256]{2,1,0:T(8,128)S(1)} %copy-done), custom_call_target="tpu_custom_call" | custom-call | tf_op jit(solution)/shard_map/orders/pallas_call | solution.py:275
  80.3 11.2 %collective-permute-done.4.refs_4_ = f32[6,256,256]{2,1,0:T(8,128)} collective-permute-done((f32[6,256,256]{2,1,0:T(8,128)}, f32[6,256,256]{2,1,0:T(8,128)}, u32[]{:S(2)}, u32[]{:S(2)}) %collective-permute-start.4) | collective-permute-done | bytes 1572896 | tf_op jit(solution)/shard_map/ppermute | solution.py:630
  91.5 4.4 %compose.1 = (f32[2,256,256]{2,1,0:T(8,128)S(1)}, f32[1,256,256]{2,1,0:T(8,128)S(1)}) custom-call(s32[18]{0:T(128)S(1)} %shard_map.166.jobs, bf16[9,256,256]{2,1,0:T(8,128)(2,1)S(1)} %orders.1.moves, f32[12,256,256]{2,1,0:T(8,128)} %bitcast.50, f32[12,256,256]{2,1,0:T(8,128)} %collective-permute-done.2.refs_1_, ...), custom_call_target="tpu_custom_call" | custom-call | tf_op jit(solution)/shard_map/compose/pallas_call | solution.py:329
  95.9 3.0 %collective-permute-start.5 = (f32[2,256,256]{2,1,0:T(8,128)S(1)}, f32[2,256,256]{2,1,0:T(8,128)S(1)}, u32[]{:S(2)}, u32[]{:S(2)}) collective-permute-start(f32[2,256,256]{2,1,0:T(8,128)S(1)} %get-tuple-element.46.refs_0_), channel_id=1, source_target_pairs={{0,8},{4,20},{8,0},{12,28},{16,24},{20,4},{24,16},{28,12},{1,9},{5... | collective-permute-start | bytes 1572872 | tf_op jit(solution)/shard_map/ppermute | solution.py:642
  98.9 1.3 collective-permute-start.11
  100.3 11.4 %collective-permute-done.5.refs_0_ = f32[2,256,256]{2,1,0:T(8,128)S(1)} collective-permute-done((f32[2,256,256]{2,1,0:T(8,128)S(1)}, f32[2,256,256]{2,1,0:T(8,128)S(1)}, u32[]{:S(2)}, u32[]{:S(2)}) %collective-permute-start.5) | collective-permute-done | bytes 524320 | tf_op jit(solution)/shard_map/ppermute | solution.py:642
  111.7 0.2 collective-permute-start.6
  112.0 0.0 collective-permute-start.14
  112.0 0.0 collective-permute-done.11.refs_1_
  112.0 0.5 collective-permute-start.13
  112.5 0.0 collective-permute-start.12
  112.5 8.4 %collective-permute-done.6.refs_0_ = f32[2,256,256]{2,1,0:T(8,128)S(1)} collective-permute-done((f32[2,256,256]{2,1,0:T(8,128)S(1)}, f32[2,256,256]{2,1,0:T(8,128)S(1)}, u32[]{:S(2)}, u32[]{:S(2)}) %collective-permute-start.6) | collective-permute-done | bytes 524320 | tf_op jit(solution)/shard_map/ppermute | solution.py:642
  120.9 0.0 collective-permute-start.7
  120.9 1.4 collective-permute-start.10
  122.3 0.0 collective-permute-start.9
  122.3 0.0 collective-permute-done.13.refs_3_
  122.3 1.0 collective-permute-start.8
  123.2 8.6 %shard_map.171 = (f32[4,8,256,256]{3,2,1,0:T(8,128)S(1)}, f32[4,8,256,256]{3,2,1,0:T(8,128)S(1)}) custom-call(s32[2]{0:T(128)S(1)} %pad_add_fusion.meta, f32[4,256,2,8,1,128]{5,4,3,2,1,0:T(1,128)} %bitcast.51, f32[4,256,2,8,1,128]{5,4,3,2,1,0:T(1,128)} %bitcast.52), custom_call_target="tpu_custom_call" | custom-call | tf_op jit(solution)/shard_map/pallas_call | solution.py:412
  131.9 10.0 %shard_map.165 = (f32[4,8,256,256]{3,2,1,0:T(8,128)S(1)}, f32[4,8,256,256]{3,2,1,0:T(8,128)S(1)}, s32[8]{0:T(128)S(1)}) custom-call(s32[2]{0:T(128)S(1)} %pad_add_fusion.meta, f32[4,256,2,8,1,128]{5,4,3,2,1,0:T(1,128)} %bitcast.53, f32[4,256,2,8,1,128]{5,4,3,2,1,0:T(1,128)} %bitcast.54), custom_call_target="tpu_custom_call" | custom-call | tf_op jit(solution)/shard_map/pallas_call | solution.py:412
  141.8 4.5 %shard_map.172 = (f32[4,8,256,256]{3,2,1,0:T(8,128)S(1)}, f32[4,8,256,256]{3,2,1,0:T(8,128)S(1)}, f32[4,8,256,256]{3,2,1,0:T(8,128)S(1)}, f32[4,8,256,256]{3,2,1...) custom-call(s32[2]{0:T(128)S(1)} %pad_add_fusion.meta, ...), custom_call_target="tpu_custom_call", output_to_operand_aliasing={{0}: (4, {}), {1}: (5, {}), {2}: (6, {}), {3}: (7, {})} | custom-call | tf_op jit(solution)/shard_map/pallas_call | solution.py:566
  146.3 0.0 collective-permute-done.12.refs_2_
  146.3 8.7 %shard_map.173 = (f32[4,8,256,256]{3,2,1,0:T(8,128)S(1)}, f32[4,8,256,256]{3,2,1,0:T(8,128)S(1)}, f32[4,8,256,256]{3,2,1,0:T(8,128)S(1)}, f32[4,8,256,256]{3,2,1...) custom-call(s32[2]{0:T(128)S(1)} %pad_add_fusion.meta, ...), custom_call_target="tpu_custom_call", output_to_operand_aliasing={{0}: (6, {}), {1}: (7, {}), {2}: (8, {}), {3}: (9, {}), {4}... | custom-call | tf_op jit(solution)/shard_map/pallas_call | solution.py:566
  155.1 0.0 collective-permute-done.9.refs_4_
  155.1 0.0 collective-permute-done.8.refs_3_
  155.1 13.0 %late.1 = (f32[4,8,256,256]{3,2,1,0:T(8,128)S(1)}, f32[4,8,256,256]{3,2,1,0:T(8,128)S(1)}, f32[4,8,256,256]{3,2,1,0:T(8,128)S(1)}, f32[4,8,256,256]{3,2,1,0:T(8,...) custom-call(s32[2]{0:T(128)S(1)} %pad_add_fusion.meta, ...), custom_call_target="tpu_custom_call", output_to_operand_aliasing={{0}: (8, {}), {1}: (9, {}), {2}: (10, {}), {3}: (11, {}), {... | custom-call | tf_op jit(solution)/shard_map/late/pallas_call | solution.py:582
  (12 shorter events, 0.1 us)
Async XLA Ops:
  0.6 6.2 %collective-permute-start.2 = (f32[12,256,256]{2,1,0:T(8,128)}, f32[12,256,256]{2,1,0:T(8,128)}, u32[]{:S(2)}, u32[]{:S(2)}) collective-permute-start(f32[12,256,256]{2,1,0:T(8,128)} %bitcast.47), channel_id=1, source_target_pairs={{0,4},{4,0},{8,12},{12,8},{16,20},{20,16},{24,28},{28,24},{1,5},{5... | collective-permute-start | bytes 9437192 | tf_op jit(solution)/shard_map/ppermute | solution.py:626
  9.5 56.9 %collective-permute-start.3 = (f32[6,256,256]{2,1,0:T(8,128)}, f32[6,256,256]{2,1,0:T(8,128)S(1)}, u32[]{:S(2)}, u32[]{:S(2)}) collective-permute-start(f32[6,256,256]{2,1,0:T(8,128)} %get-tuple-element.42), channel_id=1, source_target_pairs={{0,8},{4,20},{8,0},{12,28},{16,24},{20,4},{24,16},{28,12},{1,9},{5... | collective-permute-start | bytes 4718600 | tf_op jit(solution)/shard_map/ppermute | solution.py:630
  20.5 57.6 %copy-start = (s32[3,16,256]{2,1,0:T(8,128)S(1)}, s32[3,16,256]{2,1,0:T(8,128)}, u32[]{:S(2)}) copy-start(s32[3,16,256]{2,1,0:T(8,128)} %flags.1) | copy-start | bytes 147460
  20.5 44.3 %collective-permute-start = (f32[12,256,256]{2,1,0:T(8,128)}, f32[12,256,256]{2,1,0:T(8,128)S(1)}, u32[]{:S(2)}, u32[]{:S(2)}) collective-permute-start(f32[12,256,256]{2,1,0:T(8,128)} %param.1), channel_id=1, source_target_pairs={{0,8},{4,20},{8,0},{12,28},{16,24},{20,4},{24,16},{28,12},{1,9},{5... | collective-permute-start | bytes 9437192 | tf_op jit(solution)/shard_map/cond/branch_1_fun/ppermute | solution.py:631
  68.2 23.3 %collective-permute-start.4 = (f32[6,256,256]{2,1,0:T(8,128)}, f32[6,256,256]{2,1,0:T(8,128)}, u32[]{:S(2)}, u32[]{:S(2)}) collective-permute-start(f32[6,256,256]{2,1,0:T(8,128)} %get-tuple-element.44), channel_id=1, source_target_pairs={{0,16},{4,12},{8,24},{12,4},{16,0},{20,28},{24,8},{28,20},{1,17},{... | collective-permute-start | bytes 4718600 | tf_op jit(solution)/shard_map/ppermute | solution.py:630
  95.9 15.8 %collective-permute-start.5 = (f32[2,256,256]{2,1,0:T(8,128)S(1)}, f32[2,256,256]{2,1,0:T(8,128)S(1)}, u32[]{:S(2)}, u32[]{:S(2)}) collective-permute-start(f32[2,256,256]{2,1,0:T(8,128)S(1)} %get-tuple-element.46.refs_0_), channel_id=1, source_target_pairs={{0,8},{4,20},{8,0},{12,28},{16,24},{20,4},{24,16},{28,12},{1,9},{5... | collective-permute-start | bytes 1572872 | tf_op jit(solution)/shard_map/ppermute | solution.py:642
  98.9 13.0 %collective-permute-start.11 = (f32[2,256,256]{2,1,0:T(8,128)S(1)}, f32[2,256,256]{2,1,0:T(8,128)S(1)}, u32[]{:S(2)}, u32[]{:S(2)}) collective-permute-start(f32[2,256,256]{2,1,0:T(8,128)S(1)} %get-tuple-element.46.refs_0_), channel_id=1, source_target_pairs={{0,16},{4,12},{8,24},{12,4},{16,0},{20,28},{24,8},{28,20},{1,17},{... | collective-permute-start | bytes 1572872 | tf_op jit(solution)/shard_map/ppermute | solution.py:642
  111.7 9.2 %collective-permute-start.6 = (f32[2,256,256]{2,1,0:T(8,128)S(1)}, f32[2,256,256]{2,1,0:T(8,128)S(1)}, u32[]{:S(2)}, u32[]{:S(2)}) collective-permute-start(f32[2,256,256]{2,1,0:T(8,128)S(1)} %collective-permute-done.5.refs_0_), channel_id=1, source_target_pairs={{0,16},{4,12},{8,24},{12,4},{16,0},{20,28},{24,8},{28,20},{1,17},{... | collective-permute-start | bytes 1572872 | tf_op jit(solution)/shard_map/ppermute | solution.py:642
  112.0 10.3 %collective-permute-start.14 = (f32[2,256,256]{2,1,0:T(8,128)S(1)}, f32[2,256,256]{2,1,0:T(8,128)S(1)}, u32[]{:S(2)}, u32[]{:S(2)}) collective-permute-start(f32[2,256,256]{2,1,0:T(8,128)S(1)} %get-tuple-element.46.refs_0_), channel_id=1, source_target_pairs={{0,4},{4,0},{8,12},{12,8},{16,20},{20,16},{24,28},{28,24},{1,5},{5... | collective-permute-start | bytes 1572872 | tf_op jit(solution)/shard_map/ppermute | solution.py:640
  112.0 10.3 %collective-permute-start.13 = (f32[2,256,256]{2,1,0:T(8,128)S(1)}, f32[2,256,256]{2,1,0:T(8,128)S(1)}, u32[]{:S(2)}, u32[]{:S(2)}) collective-permute-start(f32[2,256,256]{2,1,0:T(8,128)S(1)} %collective-permute-done.11.refs_1_), channel_id=1, source_target_pairs={{0,4},{4,0},{8,12},{12,8},{16,20},{20,16},{24,28},{28,24},{1,5},{5... | collective-permute-start | bytes 1572872 | tf_op jit(solution)/shard_map/ppermute | solution.py:643
  112.5 33.9 %collective-permute-start.12 = (f32[2,256,256]{2,1,0:T(8,128)S(1)}, f32[2,256,256]{2,1,0:T(8,128)S(1)}, u32[]{:S(2)}, u32[]{:S(2)}) collective-permute-start(f32[2,256,256]{2,1,0:T(8,128)S(1)} %collective-permute-done.5.refs_0_), channel_id=1, source_target_pairs={{0,4},{4,0},{8,12},{12,8},{16,20},{20,16},{24,28},{28,24},{1,5},{5... | collective-permute-start | bytes 1572872 | tf_op jit(solution)/shard_map/ppermute | solution.py:643
  120.9 34.2 %collective-permute-start.7 = (f32[2,256,256]{2,1,0:T(8,128)S(1)}, f32[2,256,256]{2,1,0:T(8,128)S(1)}, u32[]{:S(2)}, u32[]{:S(2)}) collective-permute-start(f32[2,256,256]{2,1,0:T(8,128)S(1)} %collective-permute-done.6.refs_0_), channel_id=1, source_target_pairs={{0,4},{4,0},{8,12},{12,8},{16,20},{20,16},{24,28},{28,24},{1,5},{5... | collective-permute-start | bytes 1572872 | tf_op jit(solution)/shard_map/ppermute | solution.py:643
  120.9 34.2 %collective-permute-start.10 = (f32[1,256,256]{2,1,0:T(8,128)S(1)}, f32[1,256,256]{2,1,0:T(8,128)S(1)}, u32[]{:S(2)}, u32[]{:S(2)}) collective-permute-start(f32[1,256,256]{2,1,0:T(8,128)S(1)} %get-tuple-element.47.refs_2_), channel_id=1, source_target_pairs={{0,3},{1,0},{2,1},{3,2},{4,7},{5,4},{6,5},{7,6},{8,11},{9,8},{10,9... | collective-permute-start | bytes 786440 | tf_op jit(solution)/shard_map/ppermute | solution.py:638
  122.3 32.8 %collective-permute-start.9 = (f32[1,256,256]{2,1,0:T(8,128)S(1)}, f32[1,256,256]{2,1,0:T(8,128)S(1)}, u32[]{:S(2)}, u32[]{:S(2)}) collective-permute-start(f32[1,256,256]{2,1,0:T(8,128)S(1)} %get-tuple-element.47.refs_2_), channel_id=1, source_target_pairs={{0,2},{1,3},{2,0},{3,1},{4,6},{5,7},{6,4},{7,5},{8,10},{9,11},{10,... | collective-permute-start | bytes 786440 | tf_op jit(solution)/shard_map/ppermute | solution.py:638
  122.3 32.8 %collective-permute-start.8 = (f32[1,256,256]{2,1,0:T(8,128)S(1)}, f32[1,256,256]{2,1,0:T(8,128)S(1)}, u32[]{:S(2)}, u32[]{:S(2)}) collective-permute-start(f32[1,256,256]{2,1,0:T(8,128)S(1)} %get-tuple-element.47.refs_2_), channel_id=1, source_target_pairs={{0,1},{1,2},{2,3},{3,0},{4,5},{5,6},{6,7},{7,4},{8,9},{9,10},{10,1... | collective-permute-start | bytes 786440 | tf_op jit(solution)/shard_map/ppermute | solution.py:638

commit v2 on v1

--- a/solution.py
+++ b/solution.py
@@ -443,6 +443,13 @@
     lax.fori_loop(0, count, step, 0)
 
 
+def tallest(heights, first, count):
+    top = heights[first]
+    for step in range(1, count):
+        top = jnp.maximum(top, heights[first + step])
+    return top
+
+
 def by_height(plan, height, act):
     for count in range(1, plan.row_blocks + 1):
 
@@ -454,18 +461,16 @@
 def columns(plan, masks, meta, heights, gathered, swapped, data, outputs, high, low, places, sem):
     core, here = meta[0] % 2, meta[0] // 2
     count = jnp.int32(0)
-    slots = {}
     for index, m in enumerate(masks):
         node = here ^ combine(plan, m, core)
         base = (node * plan.col_blocks) // plan.nodes
         whole = (node * plan.col_blocks) % plan.nodes == 0
+        places[count] = base
+        count = count + whole.astype(jnp.int32)
         for unit in range(plan.col_units):
-            places[count] = base + unit
-            slots[index, unit] = count
             h, l = halves(gathered[index][unit])
             high[core, base + unit] = h
             low[core, base + unit] = l
-            count = count + whole.astype(jnp.int32)
         other = here ^ combine(plan, m, 1 - core)
         base = (other * plan.col_blocks) // plan.nodes
         for unit in range(plan.col_units):
@@ -474,19 +479,23 @@
             low[1 - core, base + unit] = l
 
     def step(index, carry):
-        b = places[index]
-        for m, kind in ((2, 0), (3, 1)):
-            ref = data[m]
-            for a in range(plan.row_blocks):
-                ref[a, b] = product(halves(ref[a, b]), (high[kind, b], low[kind, b]))
-            write_out(plan, ref, outputs[m - 2], b, sem)
+        base = places[index]
+        for unit in range(plan.col_units):
+            b = base + unit
+            for m, kind in ((2, 0), (3, 1)):
+                ref = data[m]
+                for a in range(plan.row_blocks):
+                    ref[a, b] = product(halves(ref[a, b]), (high[kind, b], low[kind, b]))
+                write_out(plan, ref, outputs[m - 2], b, sem)
 
         def pencil(height):
-            for a in range(height):
-                for m in range(2):
-                    data[m][a, b] = product(halves(data[m][a, b]), (high[1, b], low[1, b]))
-
-        by_height(plan, heights[b], pencil)
+            for unit in range(plan.col_units):
+                b = base + unit
+                for a in range(height):
+                    for m in range(2):
+                        data[m][a, b] = product(halves(data[m][a, b]), (high[1, b], low[1, b]))
+
+        by_height(plan, tallest(heights, base, plan.col_units), pencil)
         return carry
 
     lax.fori_loop(0, count, step, 0)
@@ -498,7 +507,7 @@
     gathered, swapped, refs = refs[:n], refs[n : 2 * n], refs[2 * n + 4 + extra :]
     data, outputs, (high, low, places, sem) = refs[:4], refs[4:6], refs[6:]
     count = columns(plan, masks, meta, heights, gathered, swapped, data, outputs, high, low, places, sem)
-    settle_out(plan, data[2], outputs[0], 2 * count, sem)
+    settle_out(plan, data[2], outputs[0], 2 * plan.col_units * count, sem)
 
 
 def late_kernel(plan, masks, meta, heights, *refs):
@@ -535,7 +544,7 @@
         return carry
 
     lax.fori_loop(0, plan.col_blocks, rows, 0)
-    settle_out(plan, data[0], outputs[2], 2 * count + 2 * plan.col_blocks, sem)
+    settle_out(plan, data[0], outputs[2], 2 * plan.col_units * count + 2 * plan.col_blocks, sem)
 
 
 def held_in_vmem(xs):
@@ -639,7 +648,8 @@
     gathered = [made]
     swapped = [lax.ppermute(made, "row", plan.swap())]
     for t in range(plan.stages):
-        gathered += [lax.ppermute(x, "row", plan.turn(t)) for x in gathered]
+        for m in range(1 << t):
+            gathered.append(lax.ppermute(gathered[m], "row", plan.turn(t)))
     swapped += [lax.ppermute(x, "row", plan.swap()) for x in gathered[1:]]
     last = (1 << plan.stages) - 1
     outputs = []

time: 169 us -> 167 us (0.988)
  transfers between devices with their start and end apart: 14 -> 14, of which waited for: 5 -> 5; matrix products, arithmetic and copies ran while one was open for 3% -> 3% of each run, Pallas kernels for 28% -> 27%
where the time goes in v2:
time: 167 us
  waiting for transfers between devices  77.2 us (46%)
  Pallas kernels  67.1 us (40%)
  starting transfers between devices  15.6 us (9%)
  local copies, waits for them, and re-layouts  3.19 us (2%)
  between operations  2.3 us (1%)
  other arithmetic  1.87 us (1%)
    ppermute x1, waiting for transfers between devices, steps(): sources += [moved, lax.cond(over[t], sent, lambda x: x, rest)]  44.2 us
    ppermute x3, waiting for transfers between devices, steps(): gathered.append(lax.ppermute(gathered[m], 'row', plan.turn(t)))  19.9 us
    pallas_call x2, Pallas kernels, stage(): pl.pallas_call(functools.partial(stage_kernel, plan, count), in_specs=[SM...  18.6 us
    pallas_call x1, Pallas kernels, late(): pl.pallas_call(functools.partial(late_kernel, plan, masks), in_specs=[SME...  12.6 us
    pallas_call x2, Pallas kernels, early(): pl.pallas_call(functools.partial(early_kernel, plan, masks, len(outputs))...  12.6 us
    pallas_call x3, Pallas kernels, route(): pl.pallas_call(functools.partial(route_kernel, plan, t), in_specs=[SMEM,...  12.3 us
    ppermute x2, waiting for transfers between devices, steps(): moved = sent(first)  11.2 us
    ppermute x2, starting transfers between devices, steps(): moved = sent(first)  7.47 us
  transfers between devices with their start and end apart: 14, of which 5 were waited for; matrix products, arithmetic and copies ran while one was open for 3% of the time, Pallas kernels for 27%

profile of v2, /device:TPU:0, one launch (start us, length us, event | category | flops | bytes accessed | tf_op | source)
XLA Modules:
  0.0 167.2 jit_solution(12539739136520738072)
XLA Ops:
  0.6 0.6 collective-permute-start.2
  1.2 0.1 pad_add_fusion.meta
  1.3 0.8 select_reduce_fusion
  2.0 2.9 %shard_map.167.jobs = s32[19]{0:T(128)S(1)} custom-call(s32[2]{0:T(128)S(1)} %pad_add_fusion.meta, s32[3,32]{1,0:T(4,128)S(1)} %broadcast_add_fusion.inv), custom_call_target="tpu_custom_call" | custom-call | tf_op jit(solution)/shard_map/pallas_call | solution.py:187
  4.9 1.9 %collective-permute-done.2.refs_1_ = f32[12,256,256]{2,1,0:T(8,128)} collective-permute-done((f32[12,256,256]{2,1,0:T(8,128)}, f32[12,256,256]{2,1,0:T(8,128)}, u32[]{:S(2)}, u32[]{:S(2)}) %collective-permute-start.2) | collective-permute-done | bytes 3145760 | tf_op jit(solution)/shard_map/ppermute | solution.py:635
  6.8 2.7 %shard_map.168 = (f32[6,256,256]{2,1,0:T(8,128)}, f32[12,256,256]{2,1,0:T(8,128)}) custom-call(s32[19]{0:T(128)S(1)} %shard_map.167.jobs, f32[12,256,256]{2,1,0:T(8,128)} %bitcast.48, f32[12,256,256]{2,1,0:T(8,128)} %collective-permute-done.2.refs_1_), custom_call_target="tpu_custom_call" | custom-call | tf_op jit(solution)/shard_map/pallas_call | solution.py:237
  9.5 2.9 %collective-permute-start.3 = (f32[6,256,256]{2,1,0:T(8,128)}, f32[6,256,256]{2,1,0:T(8,128)S(1)}, u32[]{:S(2)}, u32[]{:S(2)}) collective-permute-start(f32[6,256,256]{2,1,0:T(8,128)} %get-tuple-element.42), channel_id=1, source_target_pairs={{0,8},{4,20},{8,0},{12,28},{16,24},{20,4},{24,16},{28,12},{1,9},{5... | collective-permute-start | bytes 4718600 | tf_op jit(solution)/shard_map/ppermute | solution.py:639
  12.5 0.8 reshape.354
  13.2 4.8 %shard_map.169.jobs = s32[10]{0:T(128)S(1)} custom-call(s32[2]{0:T(128)S(1)} %pad_add_fusion.meta, s32[3,32]{1,0:T(4,128)S(1)} %broadcast_add_fusion.inv), custom_call_target="tpu_custom_call" | custom-call | tf_op jit(solution)/shard_map/pallas_call | solution.py:187
  18.0 0.1 xor.22
  18.2 0.9 add_reduce_fusion
  19.0 0.1 reshape.355
  19.1 0.1 reduce_max.9
  19.2 0.6 fusion.10
  20.5 0.0 copy-start
  20.5 45.9 %conditional.2 = (f32[12,256,256]{2,1,0:T(8,128)}) conditional(s32[]{:T(128)} %bitcast.9, f32[12,256,256]{2,1,0:T(8,128)} %get-tuple-element.43, f32[12,256,256]{2,1,0:T(8,128)} %get-tuple-element.43), branch_computations={%region_3.4_spmd, %region_4.5_spmd} | conditional | bytes 18874416 | solution.py:640
  20.5 0.1 collective-permute-start
  20.6 44.2 %collective-permute-done = f32[12,256,256]{2,1,0:T(8,128)S(1)} collective-permute-done((f32[12,256,256]{2,1,0:T(8,128)}, f32[12,256,256]{2,1,0:T(8,128)S(1)}, u32[]{:S(2)}, u32[]{:S(2)}) %collective-permute-start) | collective-permute-done | bytes 3145760 | tf_op jit(solution)/shard_map/cond/branch_1_fun/ppermute | solution.py:640
  64.8 1.7 copy.35
  66.4 0.0 collective-permute-done.3.refs_2_
  66.4 1.8 %shard_map.170 = (f32[6,256,256]{2,1,0:T(8,128)}, f32[3,256,256]{2,1,0:T(8,128)}) custom-call(s32[10]{0:T(128)S(1)} %shard_map.169.jobs, f32[12,256,256]{2,1,0:T(8,128)} %bitcast.49, f32[12,256,256]{2,1,0:T(8,128)} %collective-permute-done.2.refs_1_, f32[6,256,256]{2,1,0:T(8,128)S(1)} %collective-permute-done.3.refs_2_, ...), custom_call_target="tpu_custom_call" | custom-call | tf_op jit(solution)/shard_map/pallas_call | solution.py:237
  68.2 4.6 %collective-permute-start.4 = (f32[6,256,256]{2,1,0:T(8,128)}, f32[6,256,256]{2,1,0:T(8,128)}, u32[]{:S(2)}, u32[]{:S(2)}) collective-permute-start(f32[6,256,256]{2,1,0:T(8,128)} %get-tuple-element.44), channel_id=1, source_target_pairs={{0,16},{4,12},{8,24},{12,4},{16,0},{20,28},{24,8},{28,20},{1,17},{... | collective-permute-start | bytes 4718600 | tf_op jit(solution)/shard_map/ppermute | solution.py:639
  72.8 4.6 %shard_map.166.jobs = s32[18]{0:T(128)S(1)} custom-call(s32[2]{0:T(128)S(1)} %pad_add_fusion.meta, s32[3,32]{1,0:T(4,128)S(1)} %broadcast_add_fusion.inv), custom_call_target="tpu_custom_call" | custom-call | tf_op jit(solution)/shard_map/pallas_call | solution.py:187
  78.1 2.2 %orders.1.moves = bf16[9,256,256]{2,1,0:T(8,128)(2,1)S(1)} custom-call(s32[18]{0:T(128)S(1)} %shard_map.166.jobs, s32[3,16,256]{2,1,0:T(8,128)S(1)} %copy-done), custom_call_target="tpu_custom_call" | custom-call | tf_op jit(solution)/shard_map/orders/pallas_call | solution.py:275
  80.3 11.2 %collective-permute-done.4.refs_4_ = f32[6,256,256]{2,1,0:T(8,128)} collective-permute-done((f32[6,256,256]{2,1,0:T(8,128)}, f32[6,256,256]{2,1,0:T(8,128)}, u32[]{:S(2)}, u32[]{:S(2)}) %collective-permute-start.4) | collective-permute-done | bytes 1572896 | tf_op jit(solution)/shard_map/ppermute | solution.py:639
  91.5 4.4 %compose.1 = (f32[2,256,256]{2,1,0:T(8,128)S(1)}, f32[1,256,256]{2,1,0:T(8,128)S(1)}) custom-call(s32[18]{0:T(128)S(1)} %shard_map.166.jobs, bf16[9,256,256]{2,1,0:T(8,128)(2,1)S(1)} %orders.1.moves, f32[12,256,256]{2,1,0:T(8,128)} %bitcast.50, f32[12,256,256]{2,1,0:T(8,128)} %collective-permute-done.2.refs_1_, ...), custom_call_target="tpu_custom_call" | custom-call | tf_op jit(solution)/shard_map/compose/pallas_call | solution.py:329
  95.9 3.0 %collective-permute-start.5 = (f32[2,256,256]{2,1,0:T(8,128)S(1)}, f32[2,256,256]{2,1,0:T(8,128)S(1)}, u32[]{:S(2)}, u32[]{:S(2)}) collective-permute-start(f32[2,256,256]{2,1,0:T(8,128)S(1)} %get-tuple-element.46.refs_0_), channel_id=1, source_target_pairs={{0,8},{4,20},{8,0},{12,28},{16,24},{20,4},{24,16},{28,12},{1,9},{5... | collective-permute-start | bytes 1572872 | tf_op jit(solution)/shard_map/ppermute | solution.py:652
  98.9 1.3 collective-permute-start.11
  100.3 11.4 %collective-permute-done.5.refs_0_ = f32[2,256,256]{2,1,0:T(8,128)S(1)} collective-permute-done((f32[2,256,256]{2,1,0:T(8,128)S(1)}, f32[2,256,256]{2,1,0:T(8,128)S(1)}, u32[]{:S(2)}, u32[]{:S(2)}) %collective-permute-start.5) | collective-permute-done | bytes 524320 | tf_op jit(solution)/shard_map/ppermute | solution.py:652
  111.7 0.2 collective-permute-start.6
  112.0 0.0 collective-permute-done.11.refs_1_
  112.0 0.5 collective-permute-start.13
  112.5 0.0 collective-permute-start.12
  112.5 8.4 %collective-permute-done.6.refs_0_ = f32[2,256,256]{2,1,0:T(8,128)S(1)} collective-permute-done((f32[2,256,256]{2,1,0:T(8,128)S(1)}, f32[2,256,256]{2,1,0:T(8,128)S(1)}, u32[]{:S(2)}, u32[]{:S(2)}) %collective-permute-start.6) | collective-permute-done | bytes 524320 | tf_op jit(solution)/shard_map/ppermute | solution.py:652
  120.9 0.0 collective-permute-start.7
  120.9 1.4 collective-permute-start.10
  122.3 0.0 collective-permute-start.9
  122.3 0.0 collective-permute-done.13.refs_3_
  122.3 1.0 collective-permute-start.8
  123.2 8.6 %shard_map.171 = (f32[4,8,256,256]{3,2,1,0:T(8,128)S(1)}, f32[4,8,256,256]{3,2,1,0:T(8,128)S(1)}) custom-call(s32[2]{0:T(128)S(1)} %pad_add_fusion.meta, f32[4,256,2,8,1,128]{5,4,3,2,1,0:T(1,128)} %bitcast.51, f32[4,256,2,8,1,128]{5,4,3,2,1,0:T(1,128)} %bitcast.52), custom_call_target="tpu_custom_call" | custom-call | tf_op jit(solution)/shard_map/pallas_call | solution.py:412
  131.9 10.0 %shard_map.165 = (f32[4,8,256,256]{3,2,1,0:T(8,128)S(1)}, f32[4,8,256,256]{3,2,1,0:T(8,128)S(1)}, s32[8]{0:T(128)S(1)}) custom-call(s32[2]{0:T(128)S(1)} %pad_add_fusion.meta, f32[4,256,2,8,1,128]{5,4,3,2,1,0:T(1,128)} %bitcast.53, f32[4,256,2,8,1,128]{5,4,3,2,1,0:T(1,128)} %bitcast.54), custom_call_target="tpu_custom_call" | custom-call | tf_op jit(solution)/shard_map/pallas_call | solution.py:412
  141.8 4.1 %shard_map.172 = (f32[4,8,256,256]{3,2,1,0:T(8,128)S(1)}, f32[4,8,256,256]{3,2,1,0:T(8,128)S(1)}, f32[4,8,256,256]{3,2,1,0:T(8,128)S(1)}, f32[4,8,256,256]{3,2,1...) custom-call(s32[2]{0:T(128)S(1)} %pad_add_fusion.meta, ...), custom_call_target="tpu_custom_call", output_to_operand_aliasing={{0}: (4, {}), {1}: (5, {}), {2}: (6, {}), {3}: (7, {})} | custom-call | tf_op jit(solution)/shard_map/pallas_call | solution.py:575
  146.0 0.0 collective-permute-done.12.refs_2_
  146.0 8.4 %shard_map.173 = (f32[4,8,256,256]{3,2,1,0:T(8,128)S(1)}, f32[4,8,256,256]{3,2,1,0:T(8,128)S(1)}, f32[4,8,256,256]{3,2,1,0:T(8,128)S(1)}, f32[4,8,256,256]{3,2,1...) custom-call(s32[2]{0:T(128)S(1)} %pad_add_fusion.meta, ...), custom_call_target="tpu_custom_call", output_to_operand_aliasing={{0}: (6, {}), {1}: (7, {}), {2}: (8, {}), {3}: (9, {}), {4}... | custom-call | tf_op jit(solution)/shard_map/pallas_call | solution.py:575
  154.4 0.0 collective-permute-done.10.refs_5_
  154.4 0.0 collective-permute-done.8.refs_3_
  154.5 0.0 collective-permute-done.7.refs_1_
  154.5 12.6 %late.1 = (f32[4,8,256,256]{3,2,1,0:T(8,128)S(1)}, f32[4,8,256,256]{3,2,1,0:T(8,128)S(1)}, f32[4,8,256,256]{3,2,1,0:T(8,128)S(1)}, f32[4,8,256,256]{3,2,1,0:T(8,...) custom-call(s32[2]{0:T(128)S(1)} %pad_add_fusion.meta, ...), custom_call_target="tpu_custom_call", output_to_operand_aliasing={{0}: (8, {}), {1}: (9, {}), {2}: (10, {}), {3}: (11, {}), {... | custom-call | tf_op jit(solution)/shard_map/late/pallas_call | solution.py:591
  (12 shorter events, 0.1 us)
Async XLA Ops:
  0.6 6.2 %collective-permute-start.2 = (f32[12,256,256]{2,1,0:T(8,128)}, f32[12,256,256]{2,1,0:T(8,128)}, u32[]{:S(2)}, u32[]{:S(2)}) collective-permute-start(f32[12,256,256]{2,1,0:T(8,128)} %bitcast.47), channel_id=1, source_target_pairs={{0,4},{4,0},{8,12},{12,8},{16,20},{20,16},{24,28},{28,24},{1,5},{5... | collective-permute-start | bytes 9437192 | tf_op jit(solution)/shard_map/ppermute | solution.py:635
  9.5 56.9 %collective-permute-start.3 = (f32[6,256,256]{2,1,0:T(8,128)}, f32[6,256,256]{2,1,0:T(8,128)S(1)}, u32[]{:S(2)}, u32[]{:S(2)}) collective-permute-start(f32[6,256,256]{2,1,0:T(8,128)} %get-tuple-element.42), channel_id=1, source_target_pairs={{0,8},{4,20},{8,0},{12,28},{16,24},{20,4},{24,16},{28,12},{1,9},{5... | collective-permute-start | bytes 4718600 | tf_op jit(solution)/shard_map/ppermute | solution.py:639
  20.5 57.6 %copy-start = (s32[3,16,256]{2,1,0:T(8,128)S(1)}, s32[3,16,256]{2,1,0:T(8,128)}, u32[]{:S(2)}) copy-start(s32[3,16,256]{2,1,0:T(8,128)} %flags.1) | copy-start | bytes 147460
  20.5 44.3 %collective-permute-start = (f32[12,256,256]{2,1,0:T(8,128)}, f32[12,256,256]{2,1,0:T(8,128)S(1)}, u32[]{:S(2)}, u32[]{:S(2)}) collective-permute-start(f32[12,256,256]{2,1,0:T(8,128)} %param.1), channel_id=1, source_target_pairs={{0,8},{4,20},{8,0},{12,28},{16,24},{20,4},{24,16},{28,12},{1,9},{5... | collective-permute-start | bytes 9437192 | tf_op jit(solution)/shard_map/cond/branch_1_fun/ppermute | solution.py:640
  68.2 23.3 %collective-permute-start.4 = (f32[6,256,256]{2,1,0:T(8,128)}, f32[6,256,256]{2,1,0:T(8,128)}, u32[]{:S(2)}, u32[]{:S(2)}) collective-permute-start(f32[6,256,256]{2,1,0:T(8,128)} %get-tuple-element.44), channel_id=1, source_target_pairs={{0,16},{4,12},{8,24},{12,4},{16,0},{20,28},{24,8},{28,20},{1,17},{... | collective-permute-start | bytes 4718600 | tf_op jit(solution)/shard_map/ppermute | solution.py:639
  95.9 15.8 %collective-permute-start.5 = (f32[2,256,256]{2,1,0:T(8,128)S(1)}, f32[2,256,256]{2,1,0:T(8,128)S(1)}, u32[]{:S(2)}, u32[]{:S(2)}) collective-permute-start(f32[2,256,256]{2,1,0:T(8,128)S(1)} %get-tuple-element.46.refs_0_), channel_id=1, source_target_pairs={{0,8},{4,20},{8,0},{12,28},{16,24},{20,4},{24,16},{28,12},{1,9},{5... | collective-permute-start | bytes 1572872 | tf_op jit(solution)/shard_map/ppermute | solution.py:652
  98.9 13.0 %collective-permute-start.11 = (f32[2,256,256]{2,1,0:T(8,128)S(1)}, f32[2,256,256]{2,1,0:T(8,128)S(1)}, u32[]{:S(2)}, u32[]{:S(2)}) collective-permute-start(f32[2,256,256]{2,1,0:T(8,128)S(1)} %get-tuple-element.46.refs_0_), channel_id=1, source_target_pairs={{0,16},{4,12},{8,24},{12,4},{16,0},{20,28},{24,8},{28,20},{1,17},{... | collective-permute-start | bytes 1572872 | tf_op jit(solution)/shard_map/ppermute | solution.py:652
  111.7 9.2 %collective-permute-start.6 = (f32[2,256,256]{2,1,0:T(8,128)S(1)}, f32[2,256,256]{2,1,0:T(8,128)S(1)}, u32[]{:S(2)}, u32[]{:S(2)}) collective-permute-start(f32[2,256,256]{2,1,0:T(8,128)S(1)} %collective-permute-done.5.refs_0_), channel_id=1, source_target_pairs={{0,16},{4,12},{8,24},{12,4},{16,0},{20,28},{24,8},{28,20},{1,17},{... | collective-permute-start | bytes 1572872 | tf_op jit(solution)/shard_map/ppermute | solution.py:652
  112.0 10.3 %collective-permute-start.14 = (f32[2,256,256]{2,1,0:T(8,128)S(1)}, f32[2,256,256]{2,1,0:T(8,128)S(1)}, u32[]{:S(2)}, u32[]{:S(2)}) collective-permute-start(f32[2,256,256]{2,1,0:T(8,128)S(1)} %get-tuple-element.46.refs_0_), channel_id=1, source_target_pairs={{0,4},{4,0},{8,12},{12,8},{16,20},{20,16},{24,28},{28,24},{1,5},{5... | collective-permute-start | bytes 1572872 | tf_op jit(solution)/shard_map/ppermute | solution.py:649
  112.0 10.3 %collective-permute-start.13 = (f32[2,256,256]{2,1,0:T(8,128)S(1)}, f32[2,256,256]{2,1,0:T(8,128)S(1)}, u32[]{:S(2)}, u32[]{:S(2)}) collective-permute-start(f32[2,256,256]{2,1,0:T(8,128)S(1)} %collective-permute-done.11.refs_1_), channel_id=1, source_target_pairs={{0,4},{4,0},{8,12},{12,8},{16,20},{20,16},{24,28},{28,24},{1,5},{5... | collective-permute-start | bytes 1572872 | tf_op jit(solution)/shard_map/ppermute | solution.py:653
  112.5 33.5 %collective-permute-start.12 = (f32[2,256,256]{2,1,0:T(8,128)S(1)}, f32[2,256,256]{2,1,0:T(8,128)S(1)}, u32[]{:S(2)}, u32[]{:S(2)}) collective-permute-start(f32[2,256,256]{2,1,0:T(8,128)S(1)} %collective-permute-done.5.refs_0_), channel_id=1, source_target_pairs={{0,4},{4,0},{8,12},{12,8},{16,20},{20,16},{24,28},{28,24},{1,5},{5... | collective-permute-start | bytes 1572872 | tf_op jit(solution)/shard_map/ppermute | solution.py:653
  120.9 33.6 %collective-permute-start.7 = (f32[2,256,256]{2,1,0:T(8,128)S(1)}, f32[2,256,256]{2,1,0:T(8,128)S(1)}, u32[]{:S(2)}, u32[]{:S(2)}) collective-permute-start(f32[2,256,256]{2,1,0:T(8,128)S(1)} %collective-permute-done.6.refs_0_), channel_id=1, source_target_pairs={{0,4},{4,0},{8,12},{12,8},{16,20},{20,16},{24,28},{28,24},{1,5},{5... | collective-permute-start | bytes 1572872 | tf_op jit(solution)/shard_map/ppermute | solution.py:653
  120.9 33.5 %collective-permute-start.10 = (f32[1,256,256]{2,1,0:T(8,128)S(1)}, f32[1,256,256]{2,1,0:T(8,128)S(1)}, u32[]{:S(2)}, u32[]{:S(2)}) collective-permute-start(f32[1,256,256]{2,1,0:T(8,128)S(1)} %get-tuple-element.47.refs_2_), channel_id=1, source_target_pairs={{0,3},{1,0},{2,1},{3,2},{4,7},{5,4},{6,5},{7,6},{8,11},{9,8},{10,9... | collective-permute-start | bytes 786440 | tf_op jit(solution)/shard_map/ppermute | solution.py:647
  122.3 32.2 %collective-permute-start.9 = (f32[1,256,256]{2,1,0:T(8,128)S(1)}, f32[1,256,256]{2,1,0:T(8,128)S(1)}, u32[]{:S(2)}, u32[]{:S(2)}) collective-permute-start(f32[1,256,256]{2,1,0:T(8,128)S(1)} %get-tuple-element.47.refs_2_), channel_id=1, source_target_pairs={{0,2},{1,3},{2,0},{3,1},{4,6},{5,7},{6,4},{7,5},{8,10},{9,11},{10,... | collective-permute-start | bytes 786440 | tf_op jit(solution)/shard_map/ppermute | solution.py:647
  122.3 32.2 %collective-permute-start.8 = (f32[1,256,256]{2,1,0:T(8,128)S(1)}, f32[1,256,256]{2,1,0:T(8,128)S(1)}, u32[]{:S(2)}, u32[]{:S(2)}) collective-permute-start(f32[1,256,256]{2,1,0:T(8,128)S(1)} %get-tuple-element.47.refs_2_), channel_id=1, source_target_pairs={{0,1},{1,2},{2,3},{3,0},{4,5},{5,6},{6,7},{7,4},{8,9},{9,10},{10,1... | collective-permute-start | bytes 786440 | tf_op jit(solution)/shard_map/ppermute | solution.py:647
